TPU v7x, 512 devices: a whole 4x8x8 slice. The times are simulated.
512 devices in a mesh: tm: 512 (over y, z, x, core).
Axes of the slice: x: 4, y: 8, z: 8, core: 2. Of those that a mesh axis runs over, the one named last changes fastest.
Arguments:
- coupling: float32 [16384, 1536], P('tm'), may hold values from 1 to 262144, as said below
- observed: float32 [16384, 1536], P('tm'), as said below
- basis_values: float32 [384, 1536], replicated, may hold values from -0.15625 to 0.15625
Outputs:
- variance: float32 [16384, 384], P('tm')
- lag_covariance: float32 [16384, 384], P('tm')
Inputs may be any that keep to these rules, and one draw needn't show every extreme that they name: `coupling`: every entry is positive; the last row is not used. `observed`: every entry is positive.
All inputs are finite; a program needn't handle non-finite values.
Results may differ from a plain program's by a relative error of at most 0.00012.
Values sent between devices are 32-bit elements; how exact they have to be, the bound alone decides.
A program may use at most 64 MiB of HBM per device.

v0:
```python
import jax
import jax.numpy as jnp
from jax import lax
from jax.sharding import Mesh
from jax.sharding import PartitionSpec as P

TM = ("tm_0", "tm_1", "tm_2", "tm_3")


def neutral_like(shard, identity):
    return jnp.zeros_like(shard) + jnp.asarray(identity, shard.dtype)


def carried_in(shard, axes, combine, identity, reverse):
    before = start = neutral_like(shard, identity)
    running = shard
    for axis in reversed(axes):
        length, index = (lax.axis_size(axis), lax.axis_index(axis))
        pieces = lax.all_gather(running, axis)
        inside, running = (start, start)
        for k in reversed(range(length)) if reverse else range(length):
            passed = k > index if reverse else k < index
            running = combine(running, pieces[k])
            inside = jnp.where(passed, running, inside)
        before = combine(inside, before)
    return before


def mobius_join(earlier, later):
    top_left = later[0] * earlier[0] + later[1] * earlier[2]
    top_right = later[0] * earlier[1] + later[1] * earlier[3]
    low_left = later[2] * earlier[0] + later[3] * earlier[2]
    low_right = later[2] * earlier[1] + later[3] * earlier[3]
    scale_sum = top_left + top_right + low_left + low_right
    return jnp.stack([top_left, top_right, low_left, low_right]) / scale_sum


def mobius_apply(matrix, value):
    return (matrix[0] * value + matrix[1]) / (matrix[2] * value + matrix[3])


def normalized(entries):
    stacked = jnp.stack(entries)
    return stacked / jnp.sum(stacked, axis=0)


def affine_join(earlier, later):
    return jnp.stack([later[0] + later[1] * earlier[0], later[1] * earlier[1]])


def suffix_scan(combine, element_values):
    flipped = jnp.flip(element_values, axis=1)
    return jnp.flip(lax.associative_scan(combine, flipped, axis=1), axis=1)


def project(field, weights):
    return lax.dot_general(
        field,
        weights,
        (((1,), (1,)), ((), ())),
        precision=lax.Precision.HIGHEST,
        preferred_element_type=jnp.float32,
    )


def per_device(coupling, observed, basis_values):
    rows = coupling.shape[0]
    is_final = lax.axis_index(TM) == lax.axis_size(TM) - 1
    row_index_list = lax.broadcasted_iota(jnp.int32, coupling.shape, 0)
    links = jnp.where(is_final & (row_index_list == rows - 1), 0.0, coupling)
    unity = jnp.ones_like(links)
    zeros_row = jnp.zeros_like(links[0])
    half_row = 0.5 * jnp.ones_like(links[0])
    forward_steps = normalized([links, links * observed, unity, links + observed])
    prefix = lax.associative_scan(mobius_join, forward_steps, axis=1)
    forward_block = prefix[:, -1]
    forward_start = jnp.stack([half_row, zeros_row, zeros_row, half_row])
    arriving_values = carried_in(forward_block, TM, mobius_join, forward_start, False)
    first_left = arriving_values[1] / arriving_values[3]
    after_left = mobius_apply(prefix, first_left)
    left_part = jnp.concatenate([first_left[None], after_left[:-1]], axis=0)
    excess_left = observed + left_part
    pivot = links + excess_left
    ratio = links / pivot
    affine_rows = jnp.stack([1.0 / pivot, ratio * ratio])
    suffix = suffix_scan(affine_join, affine_rows)
    affine_start = jnp.stack([zeros_row, jnp.ones_like(zeros_row)])
    later_maps = carried_in(suffix[:, 0], TM, affine_join, affine_start, True)
    next_first = later_maps[0]
    variance_modes = suffix[0] + suffix[1] * next_first
    variance_next = jnp.concatenate([variance_modes[1:], next_first[None]], axis=0)
    lag_modes = ratio * variance_next
    weights = basis_values * basis_values
    return (project(variance_modes, weights), project(lag_modes, weights))


def solution(mesh):
    finer = Mesh(mesh.devices.reshape(8, 8, 4, 2), ("tm_0", "tm_1", "tm_2", "tm_3"))
    in_specs = (P(TM, None), P(TM, None), P())
    out_specs = (P(TM, None), P(TM, None))
    return jax.shard_map(
        per_device, mesh=finer, in_specs=in_specs, out_specs=out_specs, check_vma=False
    )
```

profile of v0, /device:TPU:2, one launch (start us, length us, event | category | flops | bytes accessed | tf_op | source)
XLA Modules:
  0.0 157.9 jit_solution(10896211092941609597)
XLA Ops:
  0.7 1.2 add_add_fusion
  1.9 0.1 maximum_divide_fusion
  2.1 0.2 slice.1872
  2.3 0.2 slice.1874
  3.2 0.1 slice.1910
  4.9 0.1 slice.1883
  5.3 0.2 slice.1870
  5.7 0.2 pad.695
  6.0 0.2 pad.696
  6.2 1.8 %all-gather = f32[8,1,1536]{2,1,0:T(1,128)S(1)} all-gather(f32[4,1,1536]{2,1,0:T(1,128)S(1)} %slice_add_fusion.12), channel_id=2, replica_groups=mesh['tm_0'=8,'tm_1'=8,'tm_2'=4,'tm_3'=2] {'tm_3'}, dimensions={0}, use_global_device_ids=true | all-gather | bytes 73728 | tf_op jit(solution)/shard_map/all_gather | solution.py:19
  8.6 14.6 %all_gather.37 = f32[4,4,1536]{2,1,0:T(4,128)S(1)} all-gather(f32[1,4,1536]{2,1,0:T(4,128)S(1)} %maximum_divide_fusion.12), channel_id=1, replica_groups=mesh['tm_0'=8,'tm_1'=8,'tm_2'=4,'tm_3'=2] {'tm_2'}, dimensions={0}, use_global_device_ids=true | all-gather | bytes 122880 | tf_op jit(solution)/shard_map/all_gather | solution.py:19
  23.9 28.5 %all_gather.38 = f32[8,4,1536]{2,1,0:T(4,128)S(1)} all-gather(f32[1,4,1536]{2,1,0:T(4,128)S(1)} %maximum_divide_fusion.17), channel_id=1, replica_groups=mesh['tm_0'=8,'tm_1'=8,'tm_2'=4,'tm_3'=2] {'tm_1'}, dimensions={0}, use_global_device_ids=true | all-gather | bytes 221184 | tf_op jit(solution)/shard_map/all_gather | solution.py:19
  53.2 0.3 divide_select_fusion.1
  53.6 26.3 %all_gather.39 = f32[8,4,1536]{2,1,0:T(4,128)S(1)} all-gather(f32[1,4,1536]{2,1,0:T(4,128)S(1)} %maximum_divide_fusion.26), channel_id=1, replica_groups=mesh['tm_0'=8,'tm_1'=8,'tm_2'=4,'tm_3'=2] {'tm_0'}, dimensions={0}, use_global_device_ids=true | all-gather | bytes 221184 | tf_op jit(solution)/shard_map/all_gather | solution.py:19
  80.8 0.3 divide_select_fusion
  81.4 0.2 copy-done.1
  81.7 0.8 multiply_bitcast_fusion
  82.6 0.2 slice.2161
  82.8 0.2 slice.2163
  83.2 0.2 slice.2166
  83.4 0.2 slice.2168
  85.0 1.8 %all-gather.1 = f32[4,1,1536]{2,1,0:T(1,128)S(1)} all-gather(f32[2,1,1536]{2,1,0:T(1,128)S(1)} %slice.3962), channel_id=3, replica_groups=mesh['tm_0'=8,'tm_1'=8,'tm_2'=4,'tm_3'=2] {'tm_3'}, dimensions={0}, use_global_device_ids=true | all-gather | bytes 36864 | tf_op jit(solution)/shard_map/all_gather | solution.py:19
  87.0 11.9 %all-gather.5 = f32[4,2,1536]{2,1,0:T(2,128)S(1)} all-gather(f32[1,2,1536]{2,1,0:T(2,128)S(1)} %get-tuple-element.265), channel_id=4, replica_groups=mesh['tm_0'=8,'tm_1'=8,'tm_2'=4,'tm_3'=2] {'tm_2'}, dimensions={0}, use_global_device_ids=true | all-gather | bytes 61440 | tf_op jit(solution)/shard_map/all_gather | solution.py:19
  99.0 24.6 %all-gather.6 = f32[8,2,1536]{2,1,0:T(2,128)S(1)} all-gather(f32[1,2,1536]{2,1,0:T(2,128)S(1)} %get-tuple-element.267), channel_id=5, replica_groups=mesh['tm_0'=8,'tm_1'=8,'tm_2'=4,'tm_3'=2] {'tm_1'}, dimensions={0}, use_global_device_ids=true | all-gather | bytes 110592 | tf_op jit(solution)/shard_map/all_gather | solution.py:19
  123.9 24.8 %all-gather.7 = f32[8,2,1536]{2,1,0:T(2,128)S(1)} all-gather(f32[1,2,1536]{2,1,0:T(2,128)S(1)} %fusion.57), channel_id=6, replica_groups=mesh['tm_0'=8,'tm_1'=8,'tm_2'=4,'tm_3'=2] {'tm_0'}, dimensions={0}, use_global_device_ids=true | all-gather | bytes 110592 | tf_op jit(solution)/shard_map/all_gather | solution.py:19
  149.1 0.3 slice.2156
  149.5 0.3 slice.2158
  150.1 0.2 slice.2212
  150.4 0.2 slice.2214
  150.7 0.8 copy-done
  151.5 3.7 %fusion = f32[32,384]{1,0:T(8,128)} fusion(f32[384,1536]{1,0:T(8,128)S(1)} %copy-done, f32[32,1536]{1,0:T(8,128)} %get-tuple-element.44, f32[1,1536]{1,0:T(1,128)S(1)} %get-tuple-element.3, f32[31,1536]{1,0:T(8,128)S(1)} %slice.2670), kind=kOutput, calls=%fused_computation | convolution fusion | flops 227180544 | bytes 2801664 | tf_op jit(solution)/shard_map/dot_general | solution.py:57
  155.2 2.7 %fusion.2 = f32[32,384]{1,0:T(8,128)} fusion(f32[32,1536]{1,0:T(8,128)S(1)} %fusion.8, f32[384,1536]{1,0:T(8,128)S(1)} %copy-done), kind=kOutput, calls=%fused_computation.2 | convolution fusion | flops 227082240 | bytes 2605056 | tf_op jit(solution)/shard_map/dot_general | solution.py:57
  (184 shorter events, 8.2 us)
Async XLA Ops:
  5.7 2.7 %copy-start.3 = (f32[4,1536]{1,0:T(4,128)S(1)}, f32[4,1536]{1,0:T(4,128)}, u32[]{:S(2)}) copy-start(f32[4,1536]{1,0:T(4,128)} %constant.18.clone.1) | copy-start | bytes 73732
  80.7 0.9 copy-start.1
  80.7 1.0 copy-start.2
  84.0 3.0 %copy-start.4 = (f32[2,1536]{1,0:T(2,128)S(1)}, f32[2,1536]{1,0:T(2,128)}, u32[]{:S(2)}) copy-start(f32[2,1536]{1,0:T(2,128)} %constant.51.clone.1) | copy-start | bytes 36868
  149.8 1.7 %copy-start = (f32[384,1536]{1,0:T(8,128)S(1)}, f32[384,1536]{1,0:T(8,128)}, u32[]{:S(2)}) copy-start(f32[384,1536]{1,0:T(8,128)} %param.5) | copy-start | bytes 7077892
where the time goes:
time: 158 us
  blocking collectives  134 us (85%)
  other arithmetic  8.02 us (5%)
  local copies, waits for them, and re-layouts  6.99 us (4%)
  matrix products  6.44 us (4%)
  between operations  2.17 us (1%)
    all_gather x8, blocking collectives, carried_in(): pieces = lax.all_gather(running, axis)  134 us
    dot_general x2, matrix products, project(): lax.dot_general(field, weights, (((1,), (1,)), ((), ())), precision=lax.P...  6.44 us

commit v1 on v0

v1 whole, which is shorter than its diff:
```python
import functools

import jax
import jax.numpy as jnp
from jax import lax
from jax.experimental import pallas as pl
from jax.experimental.pallas import tpu as pltpu
from jax.sharding import Mesh
from jax.sharding import PartitionSpec as P

MESH = pl.DeviceIdType.MESH
AXES = ("y", "z", "x", "c")
LANES = 128
SUB = 8
SHARE = 2


def join(a, b):
    middle = a[2] + b[0]
    inverse = 1.0 / (a[1] + b[1] + middle)
    to_left, to_right = a[1] * inverse, b[1] * inverse
    return (a[0] + to_left * middle, to_left * b[1], b[2] + to_right * middle)


def pass_right(net, value):
    seen = net[0] + value
    return net[2] + (net[1] / (net[1] + seen)) * seen


def pass_left(net, value):
    seen = net[2] + value
    return net[0] + (net[1] / (net[1] + seen)) * seen


def choose(condition, new, old):
    return tuple(jnp.where(condition, n, o) for n, o in zip(new, old))


def tree(nets):
    while len(nets) > 1:
        nets = [
            join(nets[i], nets[i + 1]) if i + 1 < len(nets) else nets[i]
            for i in range(0, len(nets), 2)
        ]
    return nets[0]


def far_first(n):
    return sorted(range(1, n), key=lambda d: -min(d, n - d))


def owned(owner, n_owners, groups):
    if n_owners == 8:
        return 3 * (owner // 2) + owner % 2, 2
    width = groups // n_owners
    return owner * width, width


def kernel(
    sizes, c_hbm, w_hbm, b_hbm, var_ref, lag_ref,
    c_v, w_v, b_v, w_high, w_low, seg, suf, pre,
    s_buf, a_buf, z_buf, y_buf, row_pre, row_suf, d_out, d_buf, stack, unmix,
    in_sem, b_sem, a_send, a_recv, z_send, z_recv, y_send, y_recv, d_send, d_recv,
):
    ny, nz, nx = sizes
    n_row = 2 * nx
    n_own = 2 * SHARE
    y, z, x, h = (lax.axis_index(a) for a in AXES)
    place = 2 * x + h
    mine = 2 * lax.rem(x, SHARE) + h
    steps, modes = c_hbm.shape
    part = steps // SUB
    groups = modes // LANES
    sites = b_v.shape[0]
    chunk = 3 * LANES
    n_chunks = modes // chunk

    loads = [
        pltpu.make_async_copy(src.at[:, pl.ds(g * LANES, LANES)], dst.at[g], in_sem.at[i, g])
        for g in range(groups)
        for i, (src, dst) in enumerate(((c_hbm, c_v), (w_hbm, w_v)))
    ]
    for load in loads:
        load.start()
    load_basis = pltpu.make_async_copy(b_hbm, b_v, b_sem)
    load_basis.start()

    row_peers = [
        (lax.rem(x + dx, nx), lax.rem(h + dh, 2))
        for dx in sorted(range(nx), key=lambda d: -min(d, nx - d))
        for dh in (0, 1)
        if dx or dh
    ]
    z_peers = [lax.rem(z + d, nz) for d in far_first(nz)]
    y_peers = [lax.rem(y + d, ny) for d in far_first(ny)]
    barrier = pltpu.get_barrier_semaphore()
    peers = (
        [(y, p, x, h) for p in z_peers]
        + [(p, z, x, h) for p in y_peers]
        + [(y, z, px, ph) for px, ph in row_peers]
    )
    for peer in peers:
        pl.semaphore_signal(barrier, inc=1, device_id=peer, device_id_type=MESH)

    is_last = (y == ny - 1) & (z == nz - 1) & (x == nx - 1) & (h == 1)
    row_index = lax.broadcasted_iota(jnp.int32, (SUB, chunk), 0)

    def step_of(buf, j, k):
        rows = pl.ds(j, SUB, stride=part)
        return jnp.concatenate([buf[g, rows, :] for g in range(3 * k, 3 * k + 3)], axis=1)

    def links_of(j, k):
        value = step_of(c_v, j, k)
        if j == part - 1:
            value = jnp.where(is_last & (row_index == SUB - 1), 0.0, value)
        return value

    for k in range(n_chunks):
        at = slice(k * chunk, (k + 1) * chunk)
        for load in loads[6 * k : 6 * k + 6]:
            load.wait()
        net = None
        for j in range(part):
            link, shunt = links_of(j, k), step_of(w_v, j, k)
            if net is None:
                net = (shunt, link, jnp.zeros_like(link))
            else:
                net = join(net, (shunt, link, jnp.zeros_like(link)))
        for p in range(3):
            seg[p, :, at] = net[p]
        for shift in (1, 2, 4):
            later = tuple(pltpu.roll(v, SUB - shift, 0) for v in net)
            net = choose(row_index + shift < SUB, join(net, later), net)
        for p in range(3):
            suf[p, :, at] = net[p]
        for q in range(n_own):
            first, width = owned(q, n_own, groups)
            for i in range(width):
                g = first + i - 3 * k
                if 0 <= g < 3:
                    for p in range(3):
                        s_buf[q, p, pl.ds(i, 1), :] = net[p][0:1, g * LANES : (g + 1) * LANES]

    sent = []

    def send(src, dst, send_sem, recv_sem, peer):
        copy = pltpu.make_async_remote_copy(
            src_ref=src, dst_ref=dst, send_sem=send_sem, recv_sem=recv_sem,
            device_id=peer, device_id_type=MESH,
        )
        copy.start()
        sent.append(copy)

    def await_slot(buf, slot, sem):
        pltpu.make_async_copy(buf.at[slot], buf.at[slot], sem.at[slot]).wait()

    def nets_of(buf, n):
        return [tuple(buf[i, p] for p in range(3)) for i in range(n)]

    pl.semaphore_wait(barrier, len(peers))
    for i, (px, ph) in enumerate(row_peers):
        target = 2 * lax.rem(px, SHARE) + ph
        send(s_buf.at[target], a_buf.at[place], a_send.at[i], a_recv.at[place], (y, z, px, ph))
    a_buf[place] = s_buf[mine]

    for k in range(n_chunks):
        at = slice(k * chunk, (k + 1) * chunk)
        net = tuple(seg[p, :, at] for p in range(3))
        for shift in (1, 2, 4):
            earlier = tuple(pltpu.roll(v, shift, 0) for v in net)
            net = choose(row_index >= shift, join(earlier, net), net)
        for p in range(3):
            pre[p, :, at] = pltpu.roll(net[p], 1, 0)
            suf[p, :, at] = pltpu.roll(suf[p, :, at], SUB - 1, 0)

    for i in range(1, n_row):
        await_slot(a_buf, lax.rem(place + i, n_row), a_recv)
    row_nets = nets_of(a_buf, n_row)
    total = tree(row_nets)
    for p in range(3):
        z_buf[z, p] = total[p]
    for i, pz in enumerate(z_peers):
        send(z_buf.at[z], z_buf.at[z], z_send.at[i], z_recv.at[z], (y, pz, x, h))

    before, after = row_nets[0], row_nets[n_row - 1]
    for i in range(1, n_row):
        for p in range(3):
            row_pre[i, p] = before[p]
            row_suf[n_row - 1 - i, p] = after[p]
        if i < n_row - 1:
            before = join(before, row_nets[i])
            after = join(row_nets[n_row - 1 - i], after)
    for p in range(3):
        row_pre[0, p] = before[p]
        row_suf[n_row - 1, p] = after[p]
    load_basis.wait()

    def weigh(i, carry):
        rows = pl.ds(pl.multiple_of(i * 16, 16), 16)
        value = b_v[rows, :]
        value = value * value
        high = value.astype(jnp.bfloat16)
        w_high[rows, :] = high
        w_low[rows, :] = (value - high.astype(jnp.float32)).astype(jnp.bfloat16)
        return carry

    lax.fori_loop(0, sites // 16, weigh, 0)

    for i in range(1, nz):
        await_slot(z_buf, lax.rem(z + i, nz), z_recv)
    z_nets = nets_of(z_buf, nz)
    total = tree(z_nets)
    for p in range(3):
        y_buf[y, p] = total[p]
    for i, py in enumerate(y_peers):
        send(y_buf.at[y], y_buf.at[y], y_send.at[i], y_recv.at[y], (py, z, x, h))
    before, after = z_nets[0], z_nets[nz - 1]
    for i in range(1, nz - 1):
        before = choose(i < z, join(before, z_nets[i]), before)
        after = choose(nz - 1 - i > z, join(z_nets[nz - 1 - i], after), after)

    for i in range(1, ny):
        await_slot(y_buf, lax.rem(y + i, ny), y_recv)
    y_nets = nets_of(y_buf, ny)
    from_left = jnp.zeros_like(y_nets[0][0])
    from_right = jnp.ones_like(from_left)
    for i in range(ny - 1):
        from_left = jnp.where(i < y, pass_right(y_nets[i], from_left), from_left)
        from_right = jnp.where(ny - 1 - i > y, pass_left(y_nets[ny - 1 - i], from_right), from_right)
    from_left = jnp.where(z > 0, pass_right(before, from_left), from_left)
    from_right = jnp.where(z < nz - 1, pass_left(after, from_right), from_right)

    base = x - lax.rem(x, SHARE)
    for i in reversed(range(n_own)):
        px, ph = base + lax.rem(lax.rem(x, SHARE) + i // 2, SHARE), lax.rem(h + i % 2, 2)
        there = 2 * px + ph
        ahead = tuple(row_pre[there, p] for p in range(3))
        behind = tuple(row_suf[there, p] for p in range(3))
        left = jnp.where(there > 0, pass_right(ahead, from_left), from_left)
        right = jnp.where(there < n_row - 1, pass_left(behind, from_right), from_right)
        if i == 0:
            d_buf[mine, 0] = left
            d_buf[mine, 1] = right
        else:
            d_out[i, 0] = left
            d_out[i, 1] = right
            send(d_out.at[i], d_buf.at[mine], d_send.at[i - 1], d_recv.at[mine], (y, z, px, ph))
    for i in range(1, n_own):
        await_slot(d_buf, lax.rem(mine + i, n_own), d_recv)

    rows = part * SUB
    for k in range(n_chunks):
        at = slice(k * chunk, (k + 1) * chunk)
        lefts, rights = [], []
        for g in range(3 * k, 3 * k + 3):
            q = next(q for q in range(n_own) if 0 <= g - owned(q, n_own, groups)[0] < owned(q, n_own, groups)[1])
            i = g - owned(q, n_own, groups)[0]
            lefts.append(jnp.broadcast_to(d_buf[q, 0, pl.ds(i, 1), :], (SUB, LANES)))
            rights.append(jnp.broadcast_to(d_buf[q, 1, pl.ds(i, 1), :], (SUB, LANES)))
        left, right = jnp.concatenate(lefts, axis=1), jnp.concatenate(rights, axis=1)
        left = jnp.where(row_index > 0, pass_right(tuple(pre[p, :, at] for p in range(3)), left), left)
        right = jnp.where(row_index < SUB - 1, pass_left(tuple(suf[p, :, at] for p in range(3)), right), right)
        inverses, ratios = [], []
        for j in range(part):
            link = links_of(j, k)
            excess = step_of(w_v, j, k) + left
            inverse = 1.0 / (link + excess)
            ratio = link * inverse
            left = ratio * excess
            inverses.append(inverse)
            ratios.append(ratio)
        variance = 1.0 / (left + right)
        variances, lags = [None] * part, [None] * part
        for j in reversed(range(part)):
            lags[j] = ratios[j] * variance
            variance = inverses[j] + ratios[j] * lags[j]
            variances[j] = variance
        field = jnp.concatenate(variances + lags, axis=0)
        high = field.astype(jnp.bfloat16)
        stack[0 : 2 * rows, at] = high
        stack[2 * rows : 4 * rows, at] = (field - high.astype(jnp.float32)).astype(jnp.bfloat16)

    contract = (((1,), (1,)), ((), ()))
    with_high = lax.dot_general(stack[...], w_high[...], contract, preferred_element_type=jnp.float32)
    with_low = lax.dot_general(stack[0 : 2 * rows, :], w_low[...], contract, preferred_element_type=jnp.float32)
    result = with_high[: 2 * rows] + (with_high[2 * rows :] + with_low)
    for o, ref in enumerate((var_ref, lag_ref)):
        for i in range(sites // LANES):
            columns = slice(i * LANES, (i + 1) * LANES)
            for j in range(part):
                first = o * rows + j * SUB
                unmix[o, i, pl.ds(j, SUB, stride=part), :] = result[first : first + SUB, columns]
            ref[:, columns] = unmix[o, i]
    for copy in sent:
        copy.wait_send()


def solution(mesh):
    ny, nz, nx = 8, 8, 4
    finer = Mesh(mesh.devices.reshape(ny, nz, nx, 2), AXES)
    return build(finer, (ny, nz, nx))


def build(finer, sizes):
    ny, nz, nx = sizes

    def per_device(coupling, observed, basis_values):
        steps, modes = coupling.shape
        sites = basis_values.shape[0]
        groups = modes // LANES
        n_row, n_own = 2 * nx, 2 * SHARE
        width = owned(0, n_own, groups)[1]
        f32 = jnp.float32
        any_spec = pl.BlockSpec(memory_space=pl.ANY)
        vmem_spec = pl.BlockSpec(memory_space=pltpu.VMEM)
        dma = pltpu.SemaphoreType.DMA
        out = jax.ShapeDtypeStruct((steps, sites), f32)
        return pl.pallas_call(
            functools.partial(kernel, sizes),
            out_shape=(out, out),
            in_specs=[any_spec] * 3,
            out_specs=(vmem_spec, vmem_spec),
            scratch_shapes=[
                pltpu.VMEM((groups, steps, LANES), f32),
                pltpu.VMEM((groups, steps, LANES), f32),
                pltpu.VMEM((sites, modes), f32),
                pltpu.VMEM((sites, modes), jnp.bfloat16),
                pltpu.VMEM((sites, modes), jnp.bfloat16),
                pltpu.VMEM((3, SUB, modes), f32),
                pltpu.VMEM((3, SUB, modes), f32),
                pltpu.VMEM((3, SUB, modes), f32),
                pltpu.VMEM((n_own, 3, width, LANES), f32),
                pltpu.VMEM((n_row, 3, width, LANES), f32),
                pltpu.VMEM((nz, 3, width, LANES), f32),
                pltpu.VMEM((ny, 3, width, LANES), f32),
                pltpu.VMEM((n_row, 3, width, LANES), f32),
                pltpu.VMEM((n_row, 3, width, LANES), f32),
                pltpu.VMEM((n_own, 2, width, LANES), f32),
                pltpu.VMEM((n_own, 2, width, LANES), f32),
                pltpu.VMEM((4 * steps, modes), jnp.bfloat16),
                pltpu.VMEM((2, sites // LANES, steps, LANES), f32),
                dma((2, groups)),
                dma,
                dma((n_row,)),
                dma((n_row,)),
                dma((nz,)),
                dma((nz,)),
                dma((ny,)),
                dma((ny,)),
                dma((n_own,)),
                dma((n_own,)),
            ],
            compiler_params=pltpu.CompilerParams(collective_id=0, has_side_effects=True),
        )(coupling, observed, basis_values)

    return jax.shard_map(
        per_device,
        mesh=finer,
        in_specs=(P(AXES, None), P(AXES, None), P()),
        out_specs=(P(AXES, None), P(AXES, None)),
        check_vma=False,
    )
```

time: 158 us -> 36.1 us (0.23)
  the two profiles are of different devices: /device:TPU:2 before, /device:TPU:1 now
where the time goes in v1:
time: 36.1 us; the launch traced here: 35.9 us
  Pallas kernels  32.4 us (90%)
  local copies, waits for them, and re-layouts  2.84 us (8%)
  between operations  0.64 us (2%)
    pallas_call x1, Pallas kernels, per_device(): pl.pallas_call(functools.partial(kernel, sizes), out_shape=(out, out), in...  32.4 us
    unnamed x2, local copies, waits for them, and re-layouts  2.84 us

profile of v1, /device:TPU:1, one launch (start us, length us, event | category | flops | bytes accessed | tf_op | source)
XLA Modules:
  0.0 35.9 jit_solution(10423122515250649657)
XLA Ops:
  0.6 32.4 %shard_map.50 = (f32[32,384]{1,0:T(8,128)}, f32[32,384]{1,0:T(8,128)}) custom-call(f32[32,1536]{1,0:T(8,128)} %c_hbm.1, f32[32,1536]{1,0:T(8,128)} %w_hbm.1, f32[384,1536]{1,0:T(8,128)} %b_hbm.1), custom_call_target="tpu_custom_call" | custom-call | tf_op jit(solution)/shard_map/pallas_call | solution.py:318
  33.0 1.4 %copy.7 = f32[32,384]{1,0:T(8,128)} copy(f32[32,384]{1,0:T(8,128)} %get-tuple-element.4) | data formatting | bytes 98304
  34.4 1.4 %copy.8 = f32[32,384]{1,0:T(8,128)} copy(f32[32,384]{1,0:T(8,128)} %get-tuple-element.5) | data formatting | bytes 98304

commit v2 on v1

--- a/solution.py
+++ b/solution.py
@@ -12,7 +12,7 @@
 AXES = ("y", "z", "x", "c")
 LANES = 128
 SUB = 8
-SHARE = 2
+SHARE = 1
 
 
 def join(a, b):
@@ -60,7 +60,7 @@
     sizes, c_hbm, w_hbm, b_hbm, var_ref, lag_ref,
     c_v, w_v, b_v, w_high, w_low, seg, suf, pre,
     s_buf, a_buf, z_buf, y_buf, row_pre, row_suf, d_out, d_buf, stack, unmix,
-    in_sem, b_sem, a_send, a_recv, z_send, z_recv, y_send, y_recv, d_send, d_recv,
+    in_sem, a_sems, z_sems, y_sems, d_sems, heard,
 ):
     ny, nz, nx = sizes
     n_row = 2 * nx
@@ -75,16 +75,6 @@
     chunk = 3 * LANES
     n_chunks = modes // chunk
 
-    loads = [
-        pltpu.make_async_copy(src.at[:, pl.ds(g * LANES, LANES)], dst.at[g], in_sem.at[i, g])
-        for g in range(groups)
-        for i, (src, dst) in enumerate(((c_hbm, c_v), (w_hbm, w_v)))
-    ]
-    for load in loads:
-        load.start()
-    load_basis = pltpu.make_async_copy(b_hbm, b_v, b_sem)
-    load_basis.start()
-
     row_peers = [
         (lax.rem(x + dx, nx), lax.rem(h + dh, 2))
         for dx in sorted(range(nx), key=lambda d: -min(d, nx - d))
@@ -93,14 +83,32 @@
     ]
     z_peers = [lax.rem(z + d, nz) for d in far_first(nz)]
     y_peers = [lax.rem(y + d, ny) for d in far_first(ny)]
+
     barrier = pltpu.get_barrier_semaphore()
-    peers = (
-        [(y, p, x, h) for p in z_peers]
-        + [(p, z, x, h) for p in y_peers]
-        + [(y, z, px, ph) for px, ph in row_peers]
-    )
-    for peer in peers:
+
+    def announce(peer):
         pl.semaphore_signal(barrier, inc=1, device_id=peer, device_id_type=MESH)
+
+    for dx in far_first(nx):
+        announce((y, z, lax.rem(x + dx, nx), 0))
+
+    @pl.when(h == 1)
+    def _():
+        announce((y, z, x, 0))
+
+    loads = [
+        pltpu.make_async_copy(src.at[:, pl.ds(g * LANES, LANES)], dst.at[g], in_sem.at[i])
+        for g in range(groups)
+        for i, (src, dst) in enumerate(((c_hbm, c_v), (w_hbm, w_v)))
+    ]
+    for load in loads:
+        load.start()
+    for p in z_peers:
+        announce((y, p, x, 1))
+    for p in y_peers:
+        announce((p, z, x, 1))
+    load_basis = pltpu.make_async_copy(b_hbm, b_v, in_sem.at[2])
+    load_basis.start()
 
     is_last = (y == ny - 1) & (z == nz - 1) & (x == nx - 1) & (h == 1)
     row_index = lax.broadcasted_iota(jnp.int32, (SUB, chunk), 0)
@@ -115,10 +123,10 @@
             value = jnp.where(is_last & (row_index == SUB - 1), 0.0, value)
         return value
 
+    for i, buf in enumerate((c_v, w_v)):
+        pltpu.make_async_copy(buf, buf, in_sem.at[i]).wait()
     for k in range(n_chunks):
         at = slice(k * chunk, (k + 1) * chunk)
-        for load in loads[6 * k : 6 * k + 6]:
-            load.wait()
         net = None
         for j in range(part):
             link, shunt = links_of(j, k), step_of(w_v, j, k)
@@ -141,26 +149,30 @@
                     for p in range(3):
                         s_buf[q, p, pl.ds(i, 1), :] = net[p][0:1, g * LANES : (g + 1) * LANES]
 
-    sent = []
-
-    def send(src, dst, send_sem, recv_sem, peer):
-        copy = pltpu.make_async_remote_copy(
-            src_ref=src, dst_ref=dst, send_sem=send_sem, recv_sem=recv_sem,
+    def send(src, dst, sems, peer):
+        pltpu.make_async_remote_copy(
+            src_ref=src, dst_ref=dst, send_sem=sems.at[0], recv_sem=sems.at[1],
             device_id=peer, device_id_type=MESH,
-        )
-        copy.start()
-        sent.append(copy)
-
-    def await_slot(buf, slot, sem):
-        pltpu.make_async_copy(buf.at[slot], buf.at[slot], sem.at[slot]).wait()
+        ).start()
+
+    def await_all(buf, n, sem):
+        pltpu.make_async_copy(buf.at[pl.ds(0, n)], buf.at[pl.ds(0, n)], sem).wait()
 
     def nets_of(buf, n):
         return [tuple(buf[i, p] for p in range(3)) for i in range(n)]
 
-    pl.semaphore_wait(barrier, len(peers))
-    for i, (px, ph) in enumerate(row_peers):
+    @pl.when(h == 0)
+    def _():
+        pl.semaphore_wait(barrier, n_row - 1)
+        pl.semaphore_signal(heard, inc=1, device_id=(y, z, x, 1), device_id_type=MESH)
+
+    @pl.when(h == 1)
+    def _():
+        pl.semaphore_wait(heard, 1)
+
+    for px, ph in row_peers:
         target = 2 * lax.rem(px, SHARE) + ph
-        send(s_buf.at[target], a_buf.at[place], a_send.at[i], a_recv.at[place], (y, z, px, ph))
+        send(s_buf.at[target], a_buf.at[place], a_sems, (y, z, px, ph))
     a_buf[place] = s_buf[mine]
 
     for k in range(n_chunks):
@@ -173,14 +185,22 @@
             pre[p, :, at] = pltpu.roll(net[p], 1, 0)
             suf[p, :, at] = pltpu.roll(suf[p, :, at], SUB - 1, 0)
 
-    for i in range(1, n_row):
-        await_slot(a_buf, lax.rem(place + i, n_row), a_recv)
+    @pl.when(h == 1)
+    def _():
+        pl.semaphore_wait(barrier, 2 * (nz - 1) + 2 * (ny - 1))
+        pl.semaphore_signal(heard, inc=1, device_id=(y, z, x, 0), device_id_type=MESH)
+
+    @pl.when(h == 0)
+    def _():
+        pl.semaphore_wait(heard, 1)
+
+    await_all(a_buf, n_row - 1, a_sems.at[1])
     row_nets = nets_of(a_buf, n_row)
     total = tree(row_nets)
     for p in range(3):
         z_buf[z, p] = total[p]
-    for i, pz in enumerate(z_peers):
-        send(z_buf.at[z], z_buf.at[z], z_send.at[i], z_recv.at[z], (y, pz, x, h))
+    for pz in z_peers:
+        send(z_buf.at[z], z_buf.at[z], z_sems, (y, pz, x, h))
 
     before, after = row_nets[0], row_nets[n_row - 1]
     for i in range(1, n_row):
@@ -206,21 +226,19 @@
 
     lax.fori_loop(0, sites // 16, weigh, 0)
 
-    for i in range(1, nz):
-        await_slot(z_buf, lax.rem(z + i, nz), z_recv)
+    await_all(z_buf, nz - 1, z_sems.at[1])
     z_nets = nets_of(z_buf, nz)
     total = tree(z_nets)
     for p in range(3):
         y_buf[y, p] = total[p]
-    for i, py in enumerate(y_peers):
-        send(y_buf.at[y], y_buf.at[y], y_send.at[i], y_recv.at[y], (py, z, x, h))
+    for py in y_peers:
+        send(y_buf.at[y], y_buf.at[y], y_sems, (py, z, x, h))
     before, after = z_nets[0], z_nets[nz - 1]
     for i in range(1, nz - 1):
         before = choose(i < z, join(before, z_nets[i]), before)
         after = choose(nz - 1 - i > z, join(z_nets[nz - 1 - i], after), after)
 
-    for i in range(1, ny):
-        await_slot(y_buf, lax.rem(y + i, ny), y_recv)
+    await_all(y_buf, ny - 1, y_sems.at[1])
     y_nets = nets_of(y_buf, ny)
     from_left = jnp.zeros_like(y_nets[0][0])
     from_right = jnp.ones_like(from_left)
@@ -244,9 +262,8 @@
         else:
             d_out[i, 0] = left
             d_out[i, 1] = right
-            send(d_out.at[i], d_buf.at[mine], d_send.at[i - 1], d_recv.at[mine], (y, z, px, ph))
-    for i in range(1, n_own):
-        await_slot(d_buf, lax.rem(mine + i, n_own), d_recv)
+            send(d_out.at[i], d_buf.at[mine], d_sems, (y, z, px, ph))
+    await_all(d_buf, n_own - 1, d_sems.at[1])
 
     rows = part * SUB
     for k in range(n_chunks):
@@ -283,16 +300,19 @@
     contract = (((1,), (1,)), ((), ()))
     with_high = lax.dot_general(stack[...], w_high[...], contract, preferred_element_type=jnp.float32)
     with_low = lax.dot_general(stack[0 : 2 * rows, :], w_low[...], contract, preferred_element_type=jnp.float32)
-    result = with_high[: 2 * rows] + (with_high[2 * rows :] + with_low)
+    parts = (with_high[: 2 * rows], with_high[2 * rows :] + with_low)
     for o, ref in enumerate((var_ref, lag_ref)):
-        for i in range(sites // LANES):
-            columns = slice(i * LANES, (i + 1) * LANES)
-            for j in range(part):
-                first = o * rows + j * SUB
-                unmix[o, i, pl.ds(j, SUB, stride=part), :] = result[first : first + SUB, columns]
-            ref[:, columns] = unmix[o, i]
-    for copy in sent:
-        copy.wait_send()
+        for b in range(2):
+            for i in range(sites // LANES):
+                columns = slice(i * LANES, (i + 1) * LANES)
+                for j in range(part):
+                    first = o * rows + j * SUB
+                    unmix[2 * o + b, i, pl.ds(j, SUB, stride=part), :] = parts[b][first : first + SUB, columns]
+                ref[b, :, columns] = unmix[2 * o + b, i]
+    await_all(a_buf, n_row - 1, a_sems.at[0])
+    await_all(z_buf, nz - 1, z_sems.at[0])
+    await_all(y_buf, ny - 1, y_sems.at[0])
+    await_all(d_buf, n_own - 1, d_sems.at[0])
 
 
 def solution(mesh):
@@ -314,8 +334,8 @@
         any_spec = pl.BlockSpec(memory_space=pl.ANY)
         vmem_spec = pl.BlockSpec(memory_space=pltpu.VMEM)
         dma = pltpu.SemaphoreType.DMA
-        out = jax.ShapeDtypeStruct((steps, sites), f32)
-        return pl.pallas_call(
+        out = pltpu.VMEM((2, steps, sites), f32)
+        fields = pl.pallas_call(
             functools.partial(kernel, sizes),
             out_shape=(out, out),
             in_specs=[any_spec] * 3,
@@ -338,20 +358,22 @@
                 pltpu.VMEM((n_own, 2, width, LANES), f32),
                 pltpu.VMEM((n_own, 2, width, LANES), f32),
                 pltpu.VMEM((4 * steps, modes), jnp.bfloat16),
-                pltpu.VMEM((2, sites // LANES, steps, LANES), f32),
-                dma((2, groups)),
-                dma,
-                dma((n_row,)),
-                dma((n_row,)),
-                dma((nz,)),
-                dma((nz,)),
-                dma((ny,)),
-                dma((ny,)),
-                dma((n_own,)),
-                dma((n_own,)),
+                pltpu.VMEM((4, sites // LANES, steps, LANES), f32),
+                dma((3,)),
+                dma((2,)),
+                dma((2,)),
+                dma((2,)),
+                dma((2,)),
+                pltpu.SemaphoreType.REGULAR,
             ],
             compiler_params=pltpu.CompilerParams(collective_id=0, has_side_effects=True),
         )(coupling, observed, basis_values)
+        zero = jnp.zeros((), f32)
+
+        def add(x, y):
+            return x[0] + y[0], x[1] + y[1]
+
+        return lax.reduce(fields, (zero, zero), add, (0,))
 
     return jax.shard_map(
         per_device,

time: 36.1 us -> 31 us (0.86)
  Pallas kernels: 32.4 us -> 29.5 us
  local copies, waits for them, and re-layouts: 2.84 us -> 0 us
  other arithmetic: 0 us -> 0.71 us
    pallas_call x1, Pallas kernels: 32.4 us -> 29.5 us  [per_device(): pl.pallas_call(functools.partial(kernel, sizes), out_shape=(out, out), in...]
    unnamed x2 -> x0, local copies, waits for them, and re-layouts: 2.84 us -> none
    another operation x0 -> x1, other arithmetic: none -> 0.71 us  [per_device(): return lax.reduce(fields, (zero, zero), add, (0,))]
where the time goes in v2:
time: 31 us; the launch traced here: 30.8 us
  Pallas kernels  29.5 us (95%)
  other arithmetic  0.71 us (2%)
  between operations  0.64 us (2%)
    pallas_call x1, Pallas kernels, per_device(): pl.pallas_call(functools.partial(kernel, sizes), out_shape=(out, out), in...  29.5 us
    another operation x1, other arithmetic, per_device(): return lax.reduce(fields, (zero, zero), add, (0,))  0.71 us

profile of v2, /device:TPU:1, one launch (start us, length us, event | category | flops | bytes accessed | tf_op | source)
XLA Modules:
  0.0 30.8 jit_solution(17368906836168321108)
XLA Ops:
  0.6 29.5 %shard_map.50 = (f32[2,32,384]{2,1,0:T(8,128)S(1)}, f32[2,32,384]{2,1,0:T(8,128)S(1)}) custom-call(f32[32,1536]{1,0:T(8,128)} %c_hbm.1, f32[32,1536]{1,0:T(8,128)} %w_hbm.1, f32[384,1536]{1,0:T(8,128)} %b_hbm.1), custom_call_target="tpu_custom_call" | custom-call | tf_op jit(solution)/shard_map/pallas_call | solution.py:338
  30.1 0.7 %reduce.15 = (f32[32,384]{1,0:T(8,128)}, f32[32,384]{1,0:T(8,128)}) reduce(f32[2,32,384]{2,1,0:T(8,128)S(1)} %get-tuple-element.4, f32[2,32,384]{2,1,0:T(8,128)S(1)} %get-tuple-element.5, f32[]{:T(128)} %constant.0.clone.1, f32[]{:T(128)} %constant.0.clone.1), dimensions={0}, to_apply=%region_0.0 | reduce | flops 24576 | bytes 294920 | tf_op jit(solution)/shard_map/reduce | solution.py:376

commit v3 on v2

v3 whole, which is shorter than its diff:
```python
import functools

import jax
import jax.numpy as jnp
from jax import lax
from jax.experimental import pallas as pl
from jax.experimental.pallas import tpu as pltpu
from jax.sharding import Mesh
from jax.sharding import PartitionSpec as P

MESH = pl.DeviceIdType.MESH
AXES = ("y", "z", "x", "c")
LANES = 128
SUB = 8


def join(a, b):
    middle = a[2] + b[0]
    inverse = 1.0 / (a[1] + b[1] + middle)
    to_left, to_right = a[1] * inverse, b[1] * inverse
    return (a[0] + to_left * middle, to_left * b[1], b[2] + to_right * middle)


def pass_right(net, value):
    seen = net[0] + value
    return net[2] + (net[1] / (net[1] + seen)) * seen


def pass_left(net, value):
    seen = net[2] + value
    return net[0] + (net[1] / (net[1] + seen)) * seen


def choose(condition, new, old):
    return tuple(jnp.where(condition, n, o) for n, o in zip(new, old))


def tree(nets):
    while len(nets) > 1:
        nets = [
            join(nets[i], nets[i + 1]) if i + 1 < len(nets) else nets[i]
            for i in range(0, len(nets), 2)
        ]
    return nets[0]


def far_first(n):
    return sorted(range(1, n), key=lambda d: -min(d, n - d))


def near_first(n):
    return sorted(range(n), key=lambda d: min(d, n - d))


def kernel(
    sizes, c_hbm, w_hbm, b_hbm, var_ref, lag_ref,
    c_v, w_v, b_v, w_high, w_low, seg, suf, pre,
    own, partner, x_buf, z_buf, y_buf, d_out, d_buf, stack, unmix,
    in_sem, p_sems, x_sems, z_sems, y_sems, d_sems,
):
    ny, nz, nx = sizes
    y, z, x, h = (lax.axis_index(a) for a in AXES)
    steps, modes = c_hbm.shape
    part = steps // SUB
    groups = modes // LANES
    sites = b_v.shape[0]
    chunk = 3 * LANES
    n_chunks = modes // chunk

    barrier = pltpu.get_barrier_semaphore()

    def announce(peer):
        pl.semaphore_signal(barrier, inc=1, device_id=peer, device_id_type=MESH)

    @pl.when(h == 1)
    def _():
        for dx in (*far_first(nx), 0):
            announce((y, z, lax.rem(x + dx, nx), 0))

    loads = [
        pltpu.make_async_copy(src.at[:, pl.ds(g * LANES, LANES)], dst.at[g], in_sem.at[i])
        for g in range(groups)
        for i, (src, dst) in enumerate(((c_hbm, c_v), (w_hbm, w_v)))
    ]
    for load in loads:
        load.start()

    @pl.when(h == 1)
    def _():
        for d in far_first(nz):
            announce((y, lax.rem(z + d, nz), x, 1))
        for d in far_first(ny):
            announce((lax.rem(y + d, ny), z, x, 1))

    load_basis = pltpu.make_async_copy(b_hbm, b_v, in_sem.at[2])
    load_basis.start()

    is_last = (y == ny - 1) & (z == nz - 1) & (x == nx - 1) & (h == 1)
    row_index = lax.broadcasted_iota(jnp.int32, (SUB, chunk), 0)

    def step_of(buf, j, k):
        rows = pl.ds(j, SUB, stride=part)
        return jnp.concatenate([buf[g, rows, :] for g in range(3 * k, 3 * k + 3)], axis=1)

    def links_of(j, k):
        value = step_of(c_v, j, k)
        if j == part - 1:
            value = jnp.where(is_last & (row_index == SUB - 1), 0.0, value)
        return value

    for i, buf in enumerate((c_v, w_v)):
        pltpu.make_async_copy(buf, buf, in_sem.at[i]).wait()
    for k in range(n_chunks):
        at = slice(k * chunk, (k + 1) * chunk)
        net = None
        for j in range(part):
            link, shunt = links_of(j, k), step_of(w_v, j, k)
            if net is None:
                net = (shunt, link, jnp.zeros_like(link))
            else:
                net = join(net, (shunt, link, jnp.zeros_like(link)))
        for p in range(3):
            seg[p, :, at] = net[p]
        for shift in (1, 2, 4):
            later = tuple(pltpu.roll(v, SUB - shift, 0) for v in net)
            net = choose(row_index + shift < SUB, join(net, later), net)
        for p in range(3):
            suf[p, :, at] = net[p]
            for g in range(3):
                own[p, pl.ds(3 * k + g, 1), :] = net[p][0:1, g * LANES : (g + 1) * LANES]

    def send(src, dst, sems, peer, known=True):
        copy = pltpu.make_async_remote_copy(
            src_ref=src, dst_ref=dst, send_sem=sems.at[0], recv_sem=sems.at[1],
            device_id=peer, device_id_type=MESH,
        )
        if known is True:
            copy.start()
        else:
            pl.when(known)(copy.start)

    def await_all(buf, n, sem):
        pltpu.make_async_copy(buf.at[pl.ds(0, n)], buf.at[pl.ds(0, n)], sem).wait()

    def await_one(buf, sem):
        pltpu.make_async_copy(buf, buf, sem).wait()

    def net_of(buf):
        return tuple(buf[p] for p in range(3))

    def nets_of(buf, n):
        return [tuple(buf[i, p] for p in range(3)) for i in range(n)]

    def around(nets, place):
        before, after = nets[0], nets[-1]
        for i in range(1, len(nets) - 1):
            before = choose(i < place, join(before, nets[i]), before)
            after = choose(len(nets) - 1 - i > place, join(nets[len(nets) - 1 - i], after), after)
        return before, after

    @pl.when(h == 0)
    def _():
        pl.semaphore_wait(barrier, nx)
        send(own, partner, p_sems, (y, z, x, 1))

    for k in range(n_chunks):
        at = slice(k * chunk, (k + 1) * chunk)
        net = tuple(seg[p, :, at] for p in range(3))
        for shift in (1, 2, 4):
            earlier = tuple(pltpu.roll(v, shift, 0) for v in net)
            net = choose(row_index >= shift, join(earlier, net), net)
        for p in range(3):
            pre[p, :, at] = pltpu.roll(net[p], 1, 0)
            suf[p, :, at] = pltpu.roll(suf[p, :, at], SUB - 1, 0)

    def weigh(i, carry):
        rows = pl.ds(pl.multiple_of(i * 16, 16), 16)
        value = b_v[rows, :]
        value = value * value
        high = value.astype(jnp.bfloat16)
        w_high[rows, :] = high
        w_low[rows, :] = (value - high.astype(jnp.float32)).astype(jnp.bfloat16)
        return carry

    blocks = sites // 16

    @pl.when(h == 1)
    def _():
        await_one(partner, p_sems.at[1])
        first, second = net_of(partner), net_of(own)
        total = join(first, second)
        for p in range(3):
            x_buf[x, p] = total[p]
        for i in range(nx):
            send(x_buf.at[x], x_buf.at[x], x_sems, (y, z, i, 1), x != i)
        pl.semaphore_wait(barrier, nz - 1 + ny - 1)
        await_all(x_buf, nx - 1, x_sems.at[1])
        x_nets = nets_of(x_buf, nx)
        total = tree(x_nets)
        for p in range(3):
            z_buf[z, p] = total[p]
        for i in range(nz // 2):
            send(z_buf.at[z], z_buf.at[z], z_sems, (y, i, x, 1), z != i)
        before_x, after_x = around(x_nets, x)
        load_basis.wait()
        lax.fori_loop(0, blocks // 2, weigh, 0)
        for i in range(nz // 2, nz):
            send(z_buf.at[z], z_buf.at[z], z_sems, (y, i, x, 1), z != i)
        await_all(z_buf, nz - 1, z_sems.at[1])
        z_nets = nets_of(z_buf, nz)
        total = tree(z_nets)
        for p in range(3):
            y_buf[y, p] = total[p]
        for i in near_first(ny)[: ny // 2 + 1]:
            send(y_buf.at[y], y_buf.at[y], y_sems, (i, z, x, 1), y != i)
        before, after = around(z_nets, z)
        before = choose(x > 0, choose(z > 0, join(before, before_x), before_x), before)
        after = choose(x < nx - 1, choose(z < nz - 1, join(after_x, after), after_x), after)
        lax.fori_loop(blocks // 2, blocks, weigh, 0)
        for i in near_first(ny)[ny // 2 + 1 :]:
            send(y_buf.at[y], y_buf.at[y], y_sems, (i, z, x, 1), y != i)
        await_all(y_buf, ny - 1, y_sems.at[1])
        y_nets = nets_of(y_buf, ny)
        from_left = jnp.zeros_like(y_nets[0][0])
        from_right = jnp.ones_like(from_left)
        for i in range(ny - 1):
            from_left = jnp.where(i < y, pass_right(y_nets[i], from_left), from_left)
            from_right = jnp.where(ny - 1 - i > y, pass_left(y_nets[ny - 1 - i], from_right), from_right)
        from_left = jnp.where((x > 0) | (z > 0), pass_right(before, from_left), from_left)
        from_right = jnp.where((x < nx - 1) | (z < nz - 1), pass_left(after, from_right), from_right)
        d_out[0] = from_left
        d_out[1] = pass_left(second, from_right)
        send(d_out, d_buf, d_sems, (y, z, x, 0))
        d_buf[0] = pass_right(first, from_left)
        d_buf[1] = from_right

    @pl.when(h == 0)
    def _():
        load_basis.wait()
        lax.fori_loop(0, blocks, weigh, 0)
        await_one(d_buf, d_sems.at[1])

    rows = part * SUB
    for k in range(n_chunks):
        at = slice(k * chunk, (k + 1) * chunk)
        left, right = (
            jnp.concatenate(
                [jnp.broadcast_to(d_buf[o, pl.ds(g, 1), :], (SUB, LANES)) for g in range(3 * k, 3 * k + 3)], axis=1
            )
            for o in range(2)
        )
        left = jnp.where(row_index > 0, pass_right(tuple(pre[p, :, at] for p in range(3)), left), left)
        right = jnp.where(row_index < SUB - 1, pass_left(tuple(suf[p, :, at] for p in range(3)), right), right)
        inverses, ratios = [], []
        for j in range(part):
            link = links_of(j, k)
            excess = step_of(w_v, j, k) + left
            inverse = 1.0 / (link + excess)
            ratio = link * inverse
            left = ratio * excess
            inverses.append(inverse)
            ratios.append(ratio)
        variance = 1.0 / (left + right)
        variances, lags = [None] * part, [None] * part
        for j in reversed(range(part)):
            lags[j] = ratios[j] * variance
            variance = inverses[j] + ratios[j] * lags[j]
            variances[j] = variance
        field = jnp.concatenate(variances + lags, axis=0)
        high = field.astype(jnp.bfloat16)
        stack[0 : 2 * rows, at] = high
        stack[2 * rows : 4 * rows, at] = (field - high.astype(jnp.float32)).astype(jnp.bfloat16)

    contract = (((1,), (1,)), ((), ()))
    with_high = lax.dot_general(stack[...], w_high[...], contract, preferred_element_type=jnp.float32)
    with_low = lax.dot_general(stack[0 : 2 * rows, :], w_low[...], contract, preferred_element_type=jnp.float32)
    parts = (with_high[: 2 * rows], with_high[2 * rows :] + with_low)
    for o, ref in enumerate((var_ref, lag_ref)):
        for b in range(2):
            for i in range(sites // LANES):
                columns = slice(i * LANES, (i + 1) * LANES)
                for j in range(part):
                    first = o * rows + j * SUB
                    unmix[2 * o + b, i, pl.ds(j, SUB, stride=part), :] = parts[b][first : first + SUB, columns]
                ref[b, :, columns] = unmix[2 * o + b, i]

    @pl.when(h == 0)
    def _():
        await_one(own, p_sems.at[0])

    @pl.when(h == 1)
    def _():
        await_all(x_buf, nx - 1, x_sems.at[0])
        await_all(z_buf, nz - 1, z_sems.at[0])
        await_all(y_buf, ny - 1, y_sems.at[0])
        await_one(d_out, d_sems.at[0])


def solution(mesh):
    ny, nz, nx = 8, 8, 4
    finer = Mesh(mesh.devices.reshape(ny, nz, nx, 2), AXES)
    return build(finer, (ny, nz, nx))


def build(finer, sizes):
    ny, nz, nx = sizes

    def per_device(coupling, observed, basis_values):
        steps, modes = coupling.shape
        sites = basis_values.shape[0]
        groups = modes // LANES
        f32 = jnp.float32
        any_spec = pl.BlockSpec(memory_space=pl.ANY)
        vmem_spec = pl.BlockSpec(memory_space=pltpu.VMEM)
        dma = pltpu.SemaphoreType.DMA
        out = pltpu.VMEM((2, steps, sites), f32)
        fields = pl.pallas_call(
            functools.partial(kernel, sizes),
            out_shape=(out, out),
            in_specs=[any_spec] * 3,
            out_specs=(vmem_spec, vmem_spec),
            scratch_shapes=[
                pltpu.VMEM((groups, steps, LANES), f32),
                pltpu.VMEM((groups, steps, LANES), f32),
                pltpu.VMEM((sites, modes), f32),
                pltpu.VMEM((sites, modes), jnp.bfloat16),
                pltpu.VMEM((sites, modes), jnp.bfloat16),
                pltpu.VMEM((3, SUB, modes), f32),
                pltpu.VMEM((3, SUB, modes), f32),
                pltpu.VMEM((3, SUB, modes), f32),
                pltpu.VMEM((3, groups, LANES), f32),
                pltpu.VMEM((3, groups, LANES), f32),
                pltpu.VMEM((nx, 3, groups, LANES), f32),
                pltpu.VMEM((nz, 3, groups, LANES), f32),
                pltpu.VMEM((ny, 3, groups, LANES), f32),
                pltpu.VMEM((2, groups, LANES), f32),
                pltpu.VMEM((2, groups, LANES), f32),
                pltpu.VMEM((4 * steps, modes), jnp.bfloat16),
                pltpu.VMEM((4, sites // LANES, steps, LANES), f32),
                dma((3,)),
                dma((2,)),
                dma((2,)),
                dma((2,)),
                dma((2,)),
                dma((2,)),
            ],
            compiler_params=pltpu.CompilerParams(collective_id=0, has_side_effects=True),
        )(coupling, observed, basis_values)
        zero = jnp.zeros((), f32)

        def add(x, y):
            return x[0] + y[0], x[1] + y[1]

        return lax.reduce(fields, (zero, zero), add, (0,))

    return jax.shard_map(
        per_device,
        mesh=finer,
        in_specs=(P(AXES, None), P(AXES, None), P()),
        out_specs=(P(AXES, None), P(AXES, None)),
        check_vma=False,
    )
```

time: 31 us -> 28.3 us (0.913)
  Pallas kernels: 29.5 us -> 26.8 us
    pallas_call x1, Pallas kernels: 29.5 us -> 26.8 us  [per_device(): pl.pallas_call(functools.partial(kernel, sizes), out_shape=(out, out), in...]
where the time goes in v3:
time: 28.3 us; the launch traced here: 28.2 us
  Pallas kernels  26.8 us (95%)
  other arithmetic  0.71 us (3%)
  between operations  0.64 us (2%)
    pallas_call x1, Pallas kernels, per_device(): pl.pallas_call(functools.partial(kernel, sizes), out_shape=(out, out), in...  26.8 us
    another operation x1, other arithmetic, per_device(): return lax.reduce(fields, (zero, zero), add, (0,))  0.71 us

profile of v3, /device:TPU:1, one launch (start us, length us, event | category | flops | bytes accessed | tf_op | source)
XLA Modules:
  0.0 28.2 jit_solution(5054228771822546332)
XLA Ops:
  0.6 26.8 %shard_map.50 = (f32[2,32,384]{2,1,0:T(8,128)S(1)}, f32[2,32,384]{2,1,0:T(8,128)S(1)}) custom-call(f32[32,1536]{1,0:T(8,128)} %c_hbm.1, f32[32,1536]{1,0:T(8,128)} %w_hbm.1, f32[384,1536]{1,0:T(8,128)} %b_hbm.1), custom_call_target="tpu_custom_call" | custom-call | tf_op jit(solution)/shard_map/pallas_call | solution.py:317
  27.5 0.7 %reduce.15 = (f32[32,384]{1,0:T(8,128)}, f32[32,384]{1,0:T(8,128)}) reduce(f32[2,32,384]{2,1,0:T(8,128)S(1)} %get-tuple-element.4, f32[2,32,384]{2,1,0:T(8,128)S(1)} %get-tuple-element.5, f32[]{:T(128)} %constant.0.clone.1, f32[]{:T(128)} %constant.0.clone.1), dimensions={0}, to_apply=%region_0.0 | reduce | flops 24576 | bytes 294920 | tf_op jit(solution)/shard_map/reduce | solution.py:354

commit v4 on v3

--- a/solution.py
+++ b/solution.py
@@ -11,6 +11,7 @@
 MESH = pl.DeviceIdType.MESH
 AXES = ("y", "z", "x", "c")
 LANES = 128
+PIECES = 2
 SUB = 8
 
 
@@ -55,7 +56,7 @@
 def kernel(
     sizes, c_hbm, w_hbm, b_hbm, var_ref, lag_ref,
     c_v, w_v, b_v, w_high, w_low, seg, suf, pre,
-    own, partner, x_buf, z_buf, y_buf, d_out, d_buf, stack, unmix,
+    own, partner, x_buf, z_buf, y_buf, sides, d_out, d_buf, stack, unmix,
     in_sem, p_sems, x_sems, z_sems, y_sems, d_sems,
 ):
     ny, nz, nx = sizes
@@ -64,8 +65,11 @@
     part = steps // SUB
     groups = modes // LANES
     sites = b_v.shape[0]
-    chunk = 3 * LANES
+    width = groups // PIECES
+    span = 3 if width % 3 == 0 else width
+    chunk = span * LANES
     n_chunks = modes // chunk
+    pieces = range(PIECES)
 
     barrier = pltpu.get_barrier_semaphore()
 
@@ -100,7 +104,7 @@
 
     def step_of(buf, j, k):
         rows = pl.ds(j, SUB, stride=part)
-        return jnp.concatenate([buf[g, rows, :] for g in range(3 * k, 3 * k + 3)], axis=1)
+        return jnp.concatenate([buf[g, rows, :] for g in range(span * k, span * k + span)], axis=1)
 
     def links_of(j, k):
         value = step_of(c_v, j, k)
@@ -126,12 +130,12 @@
             net = choose(row_index + shift < SUB, join(net, later), net)
         for p in range(3):
             suf[p, :, at] = net[p]
-            for g in range(3):
-                own[p, pl.ds(3 * k + g, 1), :] = net[p][0:1, g * LANES : (g + 1) * LANES]
-
-    def send(src, dst, sems, peer, known=True):
+            for g in range(span):
+                own[(span * k + g) // width, p, pl.ds((span * k + g) % width, 1), :] = net[p][0:1, g * LANES : (g + 1) * LANES]
+
+    def send(piece, src, dst, sems, peer, known=True):
         copy = pltpu.make_async_remote_copy(
-            src_ref=src, dst_ref=dst, send_sem=sems.at[0], recv_sem=sems.at[1],
+            src_ref=src, dst_ref=dst, send_sem=sems.at[PIECES], recv_sem=sems.at[piece],
             device_id=peer, device_id_type=MESH,
         )
         if known is True:
@@ -139,17 +143,21 @@
         else:
             pl.when(known)(copy.start)
 
-    def await_all(buf, n, sem):
-        pltpu.make_async_copy(buf.at[pl.ds(0, n)], buf.at[pl.ds(0, n)], sem).wait()
-
-    def await_one(buf, sem):
-        pltpu.make_async_copy(buf, buf, sem).wait()
-
-    def net_of(buf):
-        return tuple(buf[p] for p in range(3))
-
-    def nets_of(buf, n):
-        return [tuple(buf[i, p] for p in range(3)) for i in range(n)]
+    def await_all(piece, buf, n, sems):
+        part_of = buf.at[piece, pl.ds(0, n)]
+        pltpu.make_async_copy(part_of, part_of, sems.at[piece]).wait()
+
+    def await_one(piece, buf, sems):
+        pltpu.make_async_copy(buf.at[piece], buf.at[piece], sems.at[piece]).wait()
+
+    def await_sent(part_of, sems):
+        pltpu.make_async_copy(part_of, part_of, sems.at[PIECES]).wait()
+
+    def net_of(buf, piece):
+        return tuple(buf[piece, p] for p in range(3))
+
+    def nets_of(buf, piece, n):
+        return [tuple(buf[piece, i, p] for p in range(3)) for i in range(n)]
 
     def around(nets, place):
         before, after = nets[0], nets[-1]
@@ -161,7 +169,8 @@
     @pl.when(h == 0)
     def _():
         pl.semaphore_wait(barrier, nx)
-        send(own, partner, p_sems, (y, z, x, 1))
+        for c in pieces:
+            send(c, own.at[c], partner.at[c], p_sems, (y, z, x, 1))
 
     for k in range(n_chunks):
         at = slice(k * chunk, (k + 1) * chunk)
@@ -186,66 +195,69 @@
 
     @pl.when(h == 1)
     def _():
-        await_one(partner, p_sems.at[1])
-        first, second = net_of(partner), net_of(own)
-        total = join(first, second)
-        for p in range(3):
-            x_buf[x, p] = total[p]
-        for i in range(nx):
-            send(x_buf.at[x], x_buf.at[x], x_sems, (y, z, i, 1), x != i)
+        ends = []
+        for c in pieces:
+            await_one(c, partner, p_sems)
+            ends.append((net_of(partner, c), net_of(own, c)))
+            total = join(*ends[c])
+            for p in range(3):
+                x_buf[c, x, p] = total[p]
+            for i in range(nx):
+                send(c, x_buf.at[c, x], x_buf.at[c, x], x_sems, (y, z, i, 1), x != i)
         pl.semaphore_wait(barrier, nz - 1 + ny - 1)
-        await_all(x_buf, nx - 1, x_sems.at[1])
-        x_nets = nets_of(x_buf, nx)
-        total = tree(x_nets)
-        for p in range(3):
-            z_buf[z, p] = total[p]
-        for i in range(nz // 2):
-            send(z_buf.at[z], z_buf.at[z], z_sems, (y, i, x, 1), z != i)
-        before_x, after_x = around(x_nets, x)
+        x_nets, z_nets = [], []
+        for c in pieces:
+            await_all(c, x_buf, nx - 1, x_sems)
+            x_nets.append(nets_of(x_buf, c, nx))
+            total = tree(x_nets[c])
+            for p in range(3):
+                z_buf[c, z, p] = total[p]
+            for i in range(nz // 2):
+                send(c, z_buf.at[c, z], z_buf.at[c, z], z_sems, (y, i, x, 1), z != i)
+        row_sides = [around(x_nets[c], x) for c in pieces]
         load_basis.wait()
         lax.fori_loop(0, blocks // 2, weigh, 0)
-        for i in range(nz // 2, nz):
-            send(z_buf.at[z], z_buf.at[z], z_sems, (y, i, x, 1), z != i)
-        await_all(z_buf, nz - 1, z_sems.at[1])
-        z_nets = nets_of(z_buf, nz)
-        total = tree(z_nets)
-        for p in range(3):
-            y_buf[y, p] = total[p]
-        for i in near_first(ny)[: ny // 2 + 1]:
-            send(y_buf.at[y], y_buf.at[y], y_sems, (i, z, x, 1), y != i)
-        before, after = around(z_nets, z)
-        before = choose(x > 0, choose(z > 0, join(before, before_x), before_x), before)
-        after = choose(x < nx - 1, choose(z < nz - 1, join(after_x, after), after_x), after)
+        for c in pieces:
+            for i in range(nz // 2, nz):
+                send(c, z_buf.at[c, z], z_buf.at[c, z], z_sems, (y, i, x, 1), z != i)
+        for c in pieces:
+            await_all(c, z_buf, nz - 1, z_sems)
+            z_nets.append(nets_of(z_buf, c, nz))
+            total = tree(z_nets[c])
+            for p in range(3):
+                y_buf[c, y, p] = total[p]
+            for i in near_first(ny)[: ny // 2 + 1]:
+                send(c, y_buf.at[c, y], y_buf.at[c, y], y_sems, (i, z, x, 1), y != i)
+        for c in pieces:
+            before, after = around(z_nets[c], z)
+            before_x, after_x = row_sides[c]
+            before = choose(x > 0, choose(z > 0, join(before, before_x), before_x), before)
+            after = choose(x < nx - 1, choose(z < nz - 1, join(after_x, after), after_x), after)
+            for p in range(3):
+                sides[c, 0, p] = before[p]
+                sides[c, 1, p] = after[p]
         lax.fori_loop(blocks // 2, blocks, weigh, 0)
-        for i in near_first(ny)[ny // 2 + 1 :]:
-            send(y_buf.at[y], y_buf.at[y], y_sems, (i, z, x, 1), y != i)
-        await_all(y_buf, ny - 1, y_sems.at[1])
-        y_nets = nets_of(y_buf, ny)
-        from_left = jnp.zeros_like(y_nets[0][0])
-        from_right = jnp.ones_like(from_left)
-        for i in range(ny - 1):
-            from_left = jnp.where(i < y, pass_right(y_nets[i], from_left), from_left)
-            from_right = jnp.where(ny - 1 - i > y, pass_left(y_nets[ny - 1 - i], from_right), from_right)
-        from_left = jnp.where((x > 0) | (z > 0), pass_right(before, from_left), from_left)
-        from_right = jnp.where((x < nx - 1) | (z < nz - 1), pass_left(after, from_right), from_right)
-        d_out[0] = from_left
-        d_out[1] = pass_left(second, from_right)
-        send(d_out, d_buf, d_sems, (y, z, x, 0))
-        d_buf[0] = pass_right(first, from_left)
-        d_buf[1] = from_right
+        for c in pieces:
+            for i in near_first(ny)[ny // 2 + 1 :]:
+                send(c, y_buf.at[c, y], y_buf.at[c, y], y_sems, (i, z, x, 1), y != i)
 
     @pl.when(h == 0)
     def _():
         load_basis.wait()
         lax.fori_loop(0, blocks, weigh, 0)
-        await_one(d_buf, d_sems.at[1])
 
     rows = part * SUB
-    for k in range(n_chunks):
+    contract = (((1,), (1,)), ((), ()))
+
+    def finish(k):
         at = slice(k * chunk, (k + 1) * chunk)
         left, right = (
             jnp.concatenate(
-                [jnp.broadcast_to(d_buf[o, pl.ds(g, 1), :], (SUB, LANES)) for g in range(3 * k, 3 * k + 3)], axis=1
+                [
+                    jnp.broadcast_to(d_buf[g // width, o, pl.ds(g % width, 1), :], (SUB, LANES))
+                    for g in range(span * k, span * k + span)
+                ],
+                axis=1,
             )
             for o in range(2)
         )
@@ -271,10 +283,41 @@
         stack[0 : 2 * rows, at] = high
         stack[2 * rows : 4 * rows, at] = (field - high.astype(jnp.float32)).astype(jnp.bfloat16)
 
-    contract = (((1,), (1,)), ((), ()))
-    with_high = lax.dot_general(stack[...], w_high[...], contract, preferred_element_type=jnp.float32)
-    with_low = lax.dot_general(stack[0 : 2 * rows, :], w_low[...], contract, preferred_element_type=jnp.float32)
-    parts = (with_high[: 2 * rows], with_high[2 * rows :] + with_low)
+    parts = None
+    for c in pieces:
+        @pl.when(h == 1)
+        def _():
+            await_all(c, y_buf, ny - 1, y_sems)
+            y_nets = nets_of(y_buf, c, ny)
+            from_left = jnp.zeros_like(y_nets[0][0])
+            from_right = jnp.ones_like(from_left)
+            for i in range(ny - 1):
+                from_left = jnp.where(i < y, pass_right(y_nets[i], from_left), from_left)
+                from_right = jnp.where(ny - 1 - i > y, pass_left(y_nets[ny - 1 - i], from_right), from_right)
+            before, after = (tuple(sides[c, o, p] for p in range(3)) for o in range(2))
+            from_left = jnp.where((x > 0) | (z > 0), pass_right(before, from_left), from_left)
+            from_right = jnp.where((x < nx - 1) | (z < nz - 1), pass_left(after, from_right), from_right)
+            first, second = net_of(partner, c), net_of(own, c)
+            d_out[c, 0] = from_left
+            d_out[c, 1] = pass_left(second, from_right)
+            send(c, d_out.at[c], d_buf.at[c], d_sems, (y, z, x, 0))
+            d_buf[c, 0] = pass_right(first, from_left)
+            d_buf[c, 1] = from_right
+
+        @pl.when(h == 0)
+        def _():
+            await_one(c, d_buf, d_sems)
+
+        for k in range(c * width // span, (c + 1) * width // span):
+            finish(k)
+        at = slice(c * width * LANES, (c + 1) * width * LANES)
+        with_high = lax.dot_general(stack[:, at], w_high[:, at], contract, preferred_element_type=jnp.float32)
+        with_low = lax.dot_general(
+            stack[0 : 2 * rows, at], w_low[:, at], contract, preferred_element_type=jnp.float32
+        )
+        new = (with_high[: 2 * rows], with_high[2 * rows :] + with_low)
+        parts = new if parts is None else tuple(o + n for o, n in zip(parts, new))
+
     for o, ref in enumerate((var_ref, lag_ref)):
         for b in range(2):
             for i in range(sites // LANES):
@@ -286,14 +329,14 @@
 
     @pl.when(h == 0)
     def _():
-        await_one(own, p_sems.at[0])
+        await_sent(own, p_sems)
 
     @pl.when(h == 1)
     def _():
-        await_all(x_buf, nx - 1, x_sems.at[0])
-        await_all(z_buf, nz - 1, z_sems.at[0])
-        await_all(y_buf, ny - 1, y_sems.at[0])
-        await_one(d_out, d_sems.at[0])
+        await_sent(x_buf.at[:, pl.ds(0, nx - 1)], x_sems)
+        await_sent(z_buf.at[:, pl.ds(0, nz - 1)], z_sems)
+        await_sent(y_buf.at[:, pl.ds(0, ny - 1)], y_sems)
+        await_sent(d_out, d_sems)
 
 
 def solution(mesh):
@@ -308,6 +351,7 @@
     def per_device(coupling, observed, basis_values):
         steps, modes = coupling.shape
         sites = basis_values.shape[0]
+        width = modes // LANES // PIECES
         groups = modes // LANES
         f32 = jnp.float32
         any_spec = pl.BlockSpec(memory_space=pl.ANY)
@@ -328,21 +372,22 @@
                 pltpu.VMEM((3, SUB, modes), f32),
                 pltpu.VMEM((3, SUB, modes), f32),
                 pltpu.VMEM((3, SUB, modes), f32),
-                pltpu.VMEM((3, groups, LANES), f32),
-                pltpu.VMEM((3, groups, LANES), f32),
-                pltpu.VMEM((nx, 3, groups, LANES), f32),
-                pltpu.VMEM((nz, 3, groups, LANES), f32),
-                pltpu.VMEM((ny, 3, groups, LANES), f32),
-                pltpu.VMEM((2, groups, LANES), f32),
-                pltpu.VMEM((2, groups, LANES), f32),
+                pltpu.VMEM((PIECES, 3, width, LANES), f32),
+                pltpu.VMEM((PIECES, 3, width, LANES), f32),
+                pltpu.VMEM((PIECES, nx, 3, width, LANES), f32),
+                pltpu.VMEM((PIECES, nz, 3, width, LANES), f32),
+                pltpu.VMEM((PIECES, ny, 3, width, LANES), f32),
+                pltpu.VMEM((PIECES, 2, 3, width, LANES), f32),
+                pltpu.VMEM((PIECES, 2, width, LANES), f32),
+                pltpu.VMEM((PIECES, 2, width, LANES), f32),
                 pltpu.VMEM((4 * steps, modes), jnp.bfloat16),
                 pltpu.VMEM((4, sites // LANES, steps, LANES), f32),
                 dma((3,)),
-                dma((2,)),
-                dma((2,)),
-                dma((2,)),
-                dma((2,)),
-                dma((2,)),
+                dma((PIECES + 1,)),
+                dma((PIECES + 1,)),
+                dma((PIECES + 1,)),
+                dma((PIECES + 1,)),
+                dma((PIECES + 1,)),
             ],
             compiler_params=pltpu.CompilerParams(collective_id=0, has_side_effects=True),
         )(coupling, observed, basis_values)

time: 28.3 us -> 28.3 us (level)
  no operation moved by 1% of the time
where the time goes in v4:
time: 28.3 us; the launch traced here: 28.1 us
  Pallas kernels  26.8 us (95%)
  other arithmetic  0.71 us (3%)
  between operations  0.64 us (2%)
    pallas_call x1, Pallas kernels, per_device(): pl.pallas_call(functools.partial(kernel, sizes), out_shape=(out, out), in...  26.8 us
    another operation x1, other arithmetic, per_device(): return lax.reduce(fields, (zero, zero), add, (0,))  0.71 us

profile of v4, /device:TPU:1, one launch (start us, length us, event | category | flops | bytes accessed | tf_op | source)
XLA Modules:
  0.0 28.1 jit_solution(1219492376009201284)
XLA Ops:
  0.6 26.8 %shard_map.50 = (f32[2,32,384]{2,1,0:T(8,128)S(1)}, f32[2,32,384]{2,1,0:T(8,128)S(1)}) custom-call(f32[32,1536]{1,0:T(8,128)} %c_hbm.1, f32[32,1536]{1,0:T(8,128)} %w_hbm.1, f32[384,1536]{1,0:T(8,128)} %b_hbm.1), custom_call_target="tpu_custom_call" | custom-call | tf_op jit(solution)/shard_map/pallas_call | solution.py:361
  27.4 0.7 %reduce.15 = (f32[32,384]{1,0:T(8,128)}, f32[32,384]{1,0:T(8,128)}) reduce(f32[2,32,384]{2,1,0:T(8,128)S(1)} %get-tuple-element.4, f32[2,32,384]{2,1,0:T(8,128)S(1)} %get-tuple-element.5, f32[]{:T(128)} %constant.0.clone.1, f32[]{:T(128)} %constant.0.clone.1), dimensions={0}, to_apply=%region_0.0 | reduce | flops 24576 | bytes 294920 | tf_op jit(solution)/shard_map/reduce | solution.py:399

commit v5 on v4

--- a/solution.py
+++ b/solution.py
@@ -56,8 +56,8 @@
 def kernel(
     sizes, c_hbm, w_hbm, b_hbm, var_ref, lag_ref,
     c_v, w_v, b_v, w_high, w_low, seg, suf, pre,
-    own, partner, x_buf, z_buf, y_buf, sides, d_out, d_buf, stack, unmix,
-    in_sem, p_sems, x_sems, z_sems, y_sems, d_sems,
+    own, x_buf, z_buf, y_buf, sides, d_out, d_buf, stack, unmix,
+    in_sem, b_sem, x_sems, z_sems, y_sems, d_sems, heard,
 ):
     ny, nz, nx = sizes
     y, z, x, h = (lax.axis_index(a) for a in AXES)
@@ -82,7 +82,7 @@
             announce((y, z, lax.rem(x + dx, nx), 0))
 
     loads = [
-        pltpu.make_async_copy(src.at[:, pl.ds(g * LANES, LANES)], dst.at[g], in_sem.at[i])
+        pltpu.make_async_copy(src.at[:, pl.ds(g * LANES, LANES)], dst.at[g], in_sem.at[i, g // width])
         for g in range(groups)
         for i, (src, dst) in enumerate(((c_hbm, c_v), (w_hbm, w_v)))
     ]
@@ -96,7 +96,7 @@
         for d in far_first(ny):
             announce((lax.rem(y + d, ny), z, x, 1))
 
-    load_basis = pltpu.make_async_copy(b_hbm, b_v, in_sem.at[2])
+    load_basis = pltpu.make_async_copy(b_hbm, b_v, b_sem)
     load_basis.start()
 
     is_last = (y == ny - 1) & (z == nz - 1) & (x == nx - 1) & (h == 1)
@@ -112,10 +112,12 @@
             value = jnp.where(is_last & (row_index == SUB - 1), 0.0, value)
         return value
 
-    for i, buf in enumerate((c_v, w_v)):
-        pltpu.make_async_copy(buf, buf, in_sem.at[i]).wait()
     for k in range(n_chunks):
         at = slice(k * chunk, (k + 1) * chunk)
+        if k * span % width == 0:
+            for i, buf in enumerate((c_v, w_v)):
+                loaded = buf.at[pl.ds(k * span, width)]
+                pltpu.make_async_copy(loaded, loaded, in_sem.at[i, k * span // width]).wait()
         net = None
         for j in range(part):
             link, shunt = links_of(j, k), step_of(w_v, j, k)
@@ -169,18 +171,21 @@
     @pl.when(h == 0)
     def _():
         pl.semaphore_wait(barrier, nx)
+        pl.semaphore_signal(heard, inc=1, device_id=(y, z, x, 1), device_id_type=MESH)
         for c in pieces:
-            send(c, own.at[c], partner.at[c], p_sems, (y, z, x, 1))
-
-    for k in range(n_chunks):
-        at = slice(k * chunk, (k + 1) * chunk)
-        net = tuple(seg[p, :, at] for p in range(3))
-        for shift in (1, 2, 4):
-            earlier = tuple(pltpu.roll(v, shift, 0) for v in net)
-            net = choose(row_index >= shift, join(earlier, net), net)
-        for p in range(3):
-            pre[p, :, at] = pltpu.roll(net[p], 1, 0)
-            suf[p, :, at] = pltpu.roll(suf[p, :, at], SUB - 1, 0)
+            for d in (*far_first(nx), 0):
+                send(c, own.at[c], x_buf.at[c, 2 * x], x_sems, (y, z, lax.rem(x + d, nx), 1))
+
+    def find_prefixes():
+        for k in range(n_chunks):
+            at = slice(k * chunk, (k + 1) * chunk)
+            net = tuple(seg[p, :, at] for p in range(3))
+            for shift in (1, 2, 4):
+                earlier = tuple(pltpu.roll(v, shift, 0) for v in net)
+                net = choose(row_index >= shift, join(earlier, net), net)
+            for p in range(3):
+                pre[p, :, at] = pltpu.roll(net[p], 1, 0)
+                suf[p, :, at] = pltpu.roll(suf[p, :, at], SUB - 1, 0)
 
     def weigh(i, carry):
         rows = pl.ds(pl.multiple_of(i * 16, 16), 16)
@@ -195,39 +200,52 @@
 
     @pl.when(h == 1)
     def _():
-        ends = []
+        def spread(buf, at_place, sems, dests, peer_of):
+            for i in dests:
+                for c in pieces:
+                    send(c, buf.at[c, at_place], buf.at[c, at_place], sems, peer_of(i), at_place != i)
+
+        def spread_z(*dests):
+            spread(z_buf, z, z_sems, dests, lambda i: (y, i, x, 1))
+
+        def spread_y(*dests):
+            spread(y_buf, y, y_sems, dests, lambda i: (i, z, x, 1))
+
+        def weigh_some(i, n):
+            lax.fori_loop(blocks * i // n, blocks * (i + 1) // n, weigh, 0)
+
+        pl.semaphore_wait(heard, 1)
         for c in pieces:
-            await_one(c, partner, p_sems)
-            ends.append((net_of(partner, c), net_of(own, c)))
-            total = join(*ends[c])
             for p in range(3):
-                x_buf[c, x, p] = total[p]
-            for i in range(nx):
-                send(c, x_buf.at[c, x], x_buf.at[c, x], x_sems, (y, z, i, 1), x != i)
+                x_buf[c, 2 * x + 1, p] = own[c, p]
+            for d in far_first(nx):
+                send(c, own.at[c], x_buf.at[c, 2 * x + 1], x_sems, (y, z, lax.rem(x + d, nx), 1))
+        find_prefixes()
+        load_basis.wait()
         pl.semaphore_wait(barrier, nz - 1 + ny - 1)
         x_nets, z_nets = [], []
         for c in pieces:
-            await_all(c, x_buf, nx - 1, x_sems)
-            x_nets.append(nets_of(x_buf, c, nx))
+            await_all(c, x_buf, 2 * nx - 1, x_sems)
+            row_nets = nets_of(x_buf, c, 2 * nx)
+            x_nets.append([join(row_nets[2 * i], row_nets[2 * i + 1]) for i in range(nx)])
             total = tree(x_nets[c])
             for p in range(3):
                 z_buf[c, z, p] = total[p]
-            for i in range(nz // 2):
-                send(c, z_buf.at[c, z], z_buf.at[c, z], z_sems, (y, i, x, 1), z != i)
+            send(c, z_buf.at[c, z], z_buf.at[c, z], z_sems, (y, 0, x, 1), z != 0)
         row_sides = [around(x_nets[c], x) for c in pieces]
-        load_basis.wait()
-        lax.fori_loop(0, blocks // 2, weigh, 0)
-        for c in pieces:
-            for i in range(nz // 2, nz):
-                send(c, z_buf.at[c, z], z_buf.at[c, z], z_sems, (y, i, x, 1), z != i)
+        weigh_some(0, 6)
+        spread_z(1)
+        weigh_some(1, 6)
+        spread_z(*range(2, nz // 2))
+        weigh_some(2, 6)
+        spread_z(*range(nz // 2, nz))
         for c in pieces:
             await_all(c, z_buf, nz - 1, z_sems)
             z_nets.append(nets_of(z_buf, c, nz))
             total = tree(z_nets[c])
             for p in range(3):
                 y_buf[c, y, p] = total[p]
-            for i in near_first(ny)[: ny // 2 + 1]:
-                send(c, y_buf.at[c, y], y_buf.at[c, y], y_sems, (i, z, x, 1), y != i)
+            send(c, y_buf.at[c, y], y_buf.at[c, y], y_sems, (0, z, x, 1), y != 0)
         for c in pieces:
             before, after = around(z_nets[c], z)
             before_x, after_x = row_sides[c]
@@ -236,13 +254,18 @@
             for p in range(3):
                 sides[c, 0, p] = before[p]
                 sides[c, 1, p] = after[p]
-        lax.fori_loop(blocks // 2, blocks, weigh, 0)
-        for c in pieces:
-            for i in near_first(ny)[ny // 2 + 1 :]:
-                send(c, y_buf.at[c, y], y_buf.at[c, y], y_sems, (i, z, x, 1), y != i)
+        near = near_first(ny)
+        spread_y(*near[1:2])
+        weigh_some(3, 6)
+        spread_y(*near[2:4])
+        weigh_some(4, 6)
+        spread_y(*near[4:6])
+        weigh_some(5, 6)
+        spread_y(*near[6:])
 
     @pl.when(h == 0)
     def _():
+        find_prefixes()
         load_basis.wait()
         lax.fori_loop(0, blocks, weigh, 0)
 
@@ -297,7 +320,7 @@
             before, after = (tuple(sides[c, o, p] for p in range(3)) for o in range(2))
             from_left = jnp.where((x > 0) | (z > 0), pass_right(before, from_left), from_left)
             from_right = jnp.where((x < nx - 1) | (z < nz - 1), pass_left(after, from_right), from_right)
-            first, second = net_of(partner, c), net_of(own, c)
+            first, second = (tuple(x_buf[c, 2 * x + o, p] for p in range(3)) for o in range(2))
             d_out[c, 0] = from_left
             d_out[c, 1] = pass_left(second, from_right)
             send(c, d_out.at[c], d_buf.at[c], d_sems, (y, z, x, 0))
@@ -329,7 +352,7 @@
 
     @pl.when(h == 0)
     def _():
-        await_sent(own, p_sems)
+        await_sent(x_buf.at[:, pl.ds(0, nx)], x_sems)
 
     @pl.when(h == 1)
     def _():
@@ -373,8 +396,7 @@
                 pltpu.VMEM((3, SUB, modes), f32),
                 pltpu.VMEM((3, SUB, modes), f32),
                 pltpu.VMEM((PIECES, 3, width, LANES), f32),
-                pltpu.VMEM((PIECES, 3, width, LANES), f32),
-                pltpu.VMEM((PIECES, nx, 3, width, LANES), f32),
+                pltpu.VMEM((PIECES, 2 * nx, 3, width, LANES), f32),
                 pltpu.VMEM((PIECES, nz, 3, width, LANES), f32),
                 pltpu.VMEM((PIECES, ny, 3, width, LANES), f32),
                 pltpu.VMEM((PIECES, 2, 3, width, LANES), f32),
@@ -382,12 +404,13 @@
                 pltpu.VMEM((PIECES, 2, width, LANES), f32),
                 pltpu.VMEM((4 * steps, modes), jnp.bfloat16),
                 pltpu.VMEM((4, sites // LANES, steps, LANES), f32),
-                dma((3,)),
+                dma((2, PIECES)),
+                dma,
                 dma((PIECES + 1,)),
                 dma((PIECES + 1,)),
                 dma((PIECES + 1,)),
                 dma((PIECES + 1,)),
-                dma((PIECES + 1,)),
+                pltpu.SemaphoreType.REGULAR,
             ],
             compiler_params=pltpu.CompilerParams(collective_id=0, has_side_effects=True),
         )(coupling, observed, basis_values)

time: 28.3 us -> 27.8 us (0.982)
  Pallas kernels: 26.8 us -> 26.3 us
    pallas_call x1, Pallas kernels: 26.8 us -> 26.3 us  [per_device(): pl.pallas_call(functools.partial(kernel, sizes), out_shape=(out, out), in...]
where the time goes in v5:
time: 27.8 us; the launch traced here: 27.6 us
  Pallas kernels  26.3 us (95%)
  other arithmetic  0.71 us (3%)
  between operations  0.64 us (2%)
    pallas_call x1, Pallas kernels, per_device(): pl.pallas_call(functools.partial(kernel, sizes), out_shape=(out, out), in...  26.3 us
    another operation x1, other arithmetic, per_device(): return lax.reduce(fields, (zero, zero), add, (0,))  0.71 us

profile of v5, /device:TPU:1, one launch (start us, length us, event | category | flops | bytes accessed | tf_op | source)
XLA Modules:
  0.0 27.6 jit_solution(7558402905405214758)
XLA Ops:
  0.6 26.3 %shard_map.50 = (f32[2,32,384]{2,1,0:T(8,128)S(1)}, f32[2,32,384]{2,1,0:T(8,128)S(1)}) custom-call(f32[32,1536]{1,0:T(8,128)} %c_hbm.1, f32[32,1536]{1,0:T(8,128)} %w_hbm.1, f32[384,1536]{1,0:T(8,128)} %b_hbm.1), custom_call_target="tpu_custom_call" | custom-call | tf_op jit(solution)/shard_map/pallas_call | solution.py:384
  26.9 0.7 %reduce.15 = (f32[32,384]{1,0:T(8,128)}, f32[32,384]{1,0:T(8,128)}) reduce(f32[2,32,384]{2,1,0:T(8,128)S(1)} %get-tuple-element.4, f32[2,32,384]{2,1,0:T(8,128)S(1)} %get-tuple-element.5, f32[]{:T(128)} %constant.0.clone.1, f32[]{:T(128)} %constant.0.clone.1), dimensions={0}, to_apply=%region_0.0 | reduce | flops 24576 | bytes 294920 | tf_op jit(solution)/shard_map/reduce | solution.py:422

commit v6 on v5

--- a/solution.py
+++ b/solution.py
@@ -11,7 +11,7 @@
 MESH = pl.DeviceIdType.MESH
 AXES = ("y", "z", "x", "c")
 LANES = 128
-PIECES = 2
+PIECES = 4
 SUB = 8
 
 
@@ -55,9 +55,9 @@
 
 def kernel(
     sizes, c_hbm, w_hbm, b_hbm, var_ref, lag_ref,
-    c_v, w_v, b_v, w_high, w_low, seg, suf, pre,
-    own, x_buf, z_buf, y_buf, sides, d_out, d_buf, stack, unmix,
-    in_sem, b_sem, x_sems, z_sems, y_sems, d_sems, heard,
+    cw_v, b_v, w_high, w_low, seg, suf, pre,
+    own, nets, sides, d_out, d_buf, stack, unmix,
+    in_sem, b_sem, x_recv, z_recv, y_recv, net_sent, d_sent, heard,
 ):
     ny, nz, nx = sizes
     y, z, x, h = (lax.axis_index(a) for a in AXES)
@@ -70,6 +70,8 @@
     chunk = span * LANES
     n_chunks = modes // chunk
     pieces = range(PIECES)
+    half = groups // 2
+    at_z, at_y = 2 * nx, 2 * nx + nz
 
     barrier = pltpu.get_barrier_semaphore()
 
@@ -82,9 +84,11 @@
             announce((y, z, lax.rem(x + dx, nx), 0))
 
     loads = [
-        pltpu.make_async_copy(src.at[:, pl.ds(g * LANES, LANES)], dst.at[g], in_sem.at[i, g // width])
+        pltpu.make_async_copy(
+            src.at[:, pl.ds(g * LANES, LANES)], cw_v.at[g // half, i, g % half], in_sem.at[g // half]
+        )
         for g in range(groups)
-        for i, (src, dst) in enumerate(((c_hbm, c_v), (w_hbm, w_v)))
+        for i, src in enumerate((c_hbm, w_hbm))
     ]
     for load in loads:
         load.start()
@@ -102,25 +106,24 @@
     is_last = (y == ny - 1) & (z == nz - 1) & (x == nx - 1) & (h == 1)
     row_index = lax.broadcasted_iota(jnp.int32, (SUB, chunk), 0)
 
-    def step_of(buf, j, k):
+    def step_of(which, j, k):
         rows = pl.ds(j, SUB, stride=part)
-        return jnp.concatenate([buf[g, rows, :] for g in range(span * k, span * k + span)], axis=1)
+        return jnp.concatenate([cw_v[g // half, which, g % half, rows, :] for g in range(span * k, span * k + span)], axis=1)
 
     def links_of(j, k):
-        value = step_of(c_v, j, k)
+        value = step_of(0, j, k)
         if j == part - 1:
             value = jnp.where(is_last & (row_index == SUB - 1), 0.0, value)
         return value
 
     for k in range(n_chunks):
         at = slice(k * chunk, (k + 1) * chunk)
-        if k * span % width == 0:
-            for i, buf in enumerate((c_v, w_v)):
-                loaded = buf.at[pl.ds(k * span, width)]
-                pltpu.make_async_copy(loaded, loaded, in_sem.at[i, k * span // width]).wait()
+        if k * span % half == 0:
+            loaded = cw_v.at[k * span // half]
+            pltpu.make_async_copy(loaded, loaded, in_sem.at[k * span // half]).wait()
         net = None
         for j in range(part):
-            link, shunt = links_of(j, k), step_of(w_v, j, k)
+            link, shunt = links_of(j, k), step_of(1, j, k)
             if net is None:
                 net = (shunt, link, jnp.zeros_like(link))
             else:
@@ -135,37 +138,30 @@
             for g in range(span):
                 own[(span * k + g) // width, p, pl.ds((span * k + g) % width, 1), :] = net[p][0:1, g * LANES : (g + 1) * LANES]
 
-    def send(piece, src, dst, sems, peer, known=True):
+    def send(src, dst, sent, received, peer, known=True):
         copy = pltpu.make_async_remote_copy(
-            src_ref=src, dst_ref=dst, send_sem=sems.at[PIECES], recv_sem=sems.at[piece],
-            device_id=peer, device_id_type=MESH,
+            src_ref=src, dst_ref=dst, send_sem=sent, recv_sem=received, device_id=peer, device_id_type=MESH
         )
         if known is True:
             copy.start()
         else:
             pl.when(known)(copy.start)
 
-    def await_all(piece, buf, n, sems):
-        part_of = buf.at[piece, pl.ds(0, n)]
-        pltpu.make_async_copy(part_of, part_of, sems.at[piece]).wait()
-
-    def await_one(piece, buf, sems):
-        pltpu.make_async_copy(buf.at[piece], buf.at[piece], sems.at[piece]).wait()
-
-    def await_sent(part_of, sems):
-        pltpu.make_async_copy(part_of, part_of, sems.at[PIECES]).wait()
-
-    def net_of(buf, piece):
-        return tuple(buf[piece, p] for p in range(3))
-
-    def nets_of(buf, piece, n):
-        return [tuple(buf[piece, i, p] for p in range(3)) for i in range(n)]
-
-    def around(nets, place):
-        before, after = nets[0], nets[-1]
-        for i in range(1, len(nets) - 1):
-            before = choose(i < place, join(before, nets[i]), before)
-            after = choose(len(nets) - 1 - i > place, join(nets[len(nets) - 1 - i], after), after)
+    def await_bytes(view, sem):
+        pltpu.make_async_copy(view, view, sem).wait()
+
+    def nets_of(piece, first, n):
+        return [tuple(nets[piece, first + i, p] for p in range(3)) for i in range(n)]
+
+    def put(piece, place, net):
+        for p in range(3):
+            nets[piece, place, p] = net[p]
+
+    def around(line, place):
+        before, after = line[0], line[-1]
+        for i in range(1, len(line) - 1):
+            before = choose(i < place, join(before, line[i]), before)
+            after = choose(len(line) - 1 - i > place, join(line[len(line) - 1 - i], after), after)
         return before, after
 
     @pl.when(h == 0)
@@ -174,7 +170,7 @@
         pl.semaphore_signal(heard, inc=1, device_id=(y, z, x, 1), device_id_type=MESH)
         for c in pieces:
             for d in (*far_first(nx), 0):
-                send(c, own.at[c], x_buf.at[c, 2 * x], x_sems, (y, z, lax.rem(x + d, nx), 1))
+                send(own.at[c], nets.at[c, 2 * x], net_sent, x_recv.at[c], (y, z, lax.rem(x + d, nx), 1))
 
     def find_prefixes():
         for k in range(n_chunks):
@@ -200,52 +196,48 @@
 
     @pl.when(h == 1)
     def _():
-        def spread(buf, at_place, sems, dests, peer_of):
+        def spread(pieces, place, received, dests, peer_of):
             for i in dests:
                 for c in pieces:
-                    send(c, buf.at[c, at_place], buf.at[c, at_place], sems, peer_of(i), at_place != i)
-
-        def spread_z(*dests):
-            spread(z_buf, z, z_sems, dests, lambda i: (y, i, x, 1))
-
-        def spread_y(*dests):
-            spread(y_buf, y, y_sems, dests, lambda i: (i, z, x, 1))
+                    peer, known = peer_of(i)
+                    send(nets.at[c, place], nets.at[c, place], net_sent, received.at[c], peer, known)
+
+        def spread_z(dests, pieces=pieces):
+            spread(pieces, at_z + z, z_recv, dests, lambda i: ((y, i, x, 1), z != i))
+
+        def spread_y(dests, pieces=pieces):
+            spread(pieces, at_y + y, y_recv, dests, lambda i: ((i, z, x, 1), y != i))
 
         def weigh_some(i, n):
             lax.fori_loop(blocks * i // n, blocks * (i + 1) // n, weigh, 0)
 
         pl.semaphore_wait(heard, 1)
         for c in pieces:
-            for p in range(3):
-                x_buf[c, 2 * x + 1, p] = own[c, p]
+            put(c, 2 * x + 1, own[c])
             for d in far_first(nx):
-                send(c, own.at[c], x_buf.at[c, 2 * x + 1], x_sems, (y, z, lax.rem(x + d, nx), 1))
+                send(own.at[c], nets.at[c, 2 * x + 1], net_sent, x_recv.at[c], (y, z, lax.rem(x + d, nx), 1))
         find_prefixes()
         load_basis.wait()
         pl.semaphore_wait(barrier, nz - 1 + ny - 1)
         x_nets, z_nets = [], []
         for c in pieces:
-            await_all(c, x_buf, 2 * nx - 1, x_sems)
-            row_nets = nets_of(x_buf, c, 2 * nx)
+            await_bytes(nets.at[c, pl.ds(0, 2 * nx - 1)], x_recv.at[c])
+            row_nets = nets_of(c, 0, 2 * nx)
             x_nets.append([join(row_nets[2 * i], row_nets[2 * i + 1]) for i in range(nx)])
-            total = tree(x_nets[c])
-            for p in range(3):
-                z_buf[c, z, p] = total[p]
-            send(c, z_buf.at[c, z], z_buf.at[c, z], z_sems, (y, 0, x, 1), z != 0)
+            put(c, at_z + z, tree(x_nets[c]))
+            spread_z((0,), (c,))
         row_sides = [around(x_nets[c], x) for c in pieces]
         weigh_some(0, 6)
-        spread_z(1)
+        spread_z((1,))
         weigh_some(1, 6)
-        spread_z(*range(2, nz // 2))
+        spread_z(range(2, nz // 2))
         weigh_some(2, 6)
-        spread_z(*range(nz // 2, nz))
+        spread_z(range(nz // 2, nz))
         for c in pieces:
-            await_all(c, z_buf, nz - 1, z_sems)
-            z_nets.append(nets_of(z_buf, c, nz))
-            total = tree(z_nets[c])
-            for p in range(3):
-                y_buf[c, y, p] = total[p]
-            send(c, y_buf.at[c, y], y_buf.at[c, y], y_sems, (0, z, x, 1), y != 0)
+            await_bytes(nets.at[c, pl.ds(at_z, nz - 1)], z_recv.at[c])
+            z_nets.append(nets_of(c, at_z, nz))
+            put(c, at_y + y, tree(z_nets[c]))
+            spread_y((0,), (c,))
         for c in pieces:
             before, after = around(z_nets[c], z)
             before_x, after_x = row_sides[c]
@@ -255,13 +247,13 @@
                 sides[c, 0, p] = before[p]
                 sides[c, 1, p] = after[p]
         near = near_first(ny)
-        spread_y(*near[1:2])
+        spread_y(near[1:2])
         weigh_some(3, 6)
-        spread_y(*near[2:4])
+        spread_y(near[2:4])
         weigh_some(4, 6)
-        spread_y(*near[4:6])
+        spread_y(near[4:6])
         weigh_some(5, 6)
-        spread_y(*near[6:])
+        spread_y(near[6:])
 
     @pl.when(h == 0)
     def _():
@@ -289,7 +281,7 @@
         inverses, ratios = [], []
         for j in range(part):
             link = links_of(j, k)
-            excess = step_of(w_v, j, k) + left
+            excess = step_of(1, j, k) + left
             inverse = 1.0 / (link + excess)
             ratio = link * inverse
             left = ratio * excess
@@ -306,12 +298,11 @@
         stack[0 : 2 * rows, at] = high
         stack[2 * rows : 4 * rows, at] = (field - high.astype(jnp.float32)).astype(jnp.bfloat16)
 
-    parts = None
-    for c in pieces:
+    def learn(c):
         @pl.when(h == 1)
         def _():
-            await_all(c, y_buf, ny - 1, y_sems)
-            y_nets = nets_of(y_buf, c, ny)
+            await_bytes(nets.at[c, pl.ds(at_y, ny - 1)], y_recv.at[c])
+            y_nets = nets_of(c, at_y, ny)
             from_left = jnp.zeros_like(y_nets[0][0])
             from_right = jnp.ones_like(from_left)
             for i in range(ny - 1):
@@ -320,26 +311,33 @@
             before, after = (tuple(sides[c, o, p] for p in range(3)) for o in range(2))
             from_left = jnp.where((x > 0) | (z > 0), pass_right(before, from_left), from_left)
             from_right = jnp.where((x < nx - 1) | (z < nz - 1), pass_left(after, from_right), from_right)
-            first, second = (tuple(x_buf[c, 2 * x + o, p] for p in range(3)) for o in range(2))
+            first, second = (tuple(nets[c, 2 * x + o, p] for p in range(3)) for o in range(2))
             d_out[c, 0] = from_left
             d_out[c, 1] = pass_left(second, from_right)
-            send(c, d_out.at[c], d_buf.at[c], d_sems, (y, z, x, 0))
+            send(d_out.at[c], d_buf.at[c], d_sent, x_recv.at[c], (y, z, x, 0))
             d_buf[c, 0] = pass_right(first, from_left)
             d_buf[c, 1] = from_right
 
         @pl.when(h == 0)
         def _():
-            await_one(c, d_buf, d_sems)
-
-        for k in range(c * width // span, (c + 1) * width // span):
-            finish(k)
-        at = slice(c * width * LANES, (c + 1) * width * LANES)
+            await_bytes(d_buf.at[c], x_recv.at[c])
+
+    def multiply(i):
+        at = slice(i * half * LANES, (i + 1) * half * LANES)
         with_high = lax.dot_general(stack[:, at], w_high[:, at], contract, preferred_element_type=jnp.float32)
         with_low = lax.dot_general(
             stack[0 : 2 * rows, at], w_low[:, at], contract, preferred_element_type=jnp.float32
         )
-        new = (with_high[: 2 * rows], with_high[2 * rows :] + with_low)
-        parts = new if parts is None else tuple(o + n for o, n in zip(parts, new))
+        return with_high[: 2 * rows], with_high[2 * rows :] + with_low
+
+    parts = None
+    for c in pieces:
+        learn(c)
+        for k in range(c * width // span, (c + 1) * width // span):
+            finish(k)
+        if (c + 1) * width % half == 0:
+            new = multiply(c * width // half)
+            parts = new if parts is None else tuple(o + n for o, n in zip(parts, new))
 
     for o, ref in enumerate((var_ref, lag_ref)):
         for b in range(2):
@@ -352,14 +350,12 @@
 
     @pl.when(h == 0)
     def _():
-        await_sent(x_buf.at[:, pl.ds(0, nx)], x_sems)
+        await_bytes(nets.at[:, pl.ds(0, nx)], net_sent)
 
     @pl.when(h == 1)
     def _():
-        await_sent(x_buf.at[:, pl.ds(0, nx - 1)], x_sems)
-        await_sent(z_buf.at[:, pl.ds(0, nz - 1)], z_sems)
-        await_sent(y_buf.at[:, pl.ds(0, ny - 1)], y_sems)
-        await_sent(d_out, d_sems)
+        await_bytes(nets.at[:, pl.ds(0, nx - 1 + nz - 1 + ny - 1)], net_sent)
+        await_bytes(d_out, d_sent)
 
 
 def solution(mesh):
@@ -387,8 +383,7 @@
             in_specs=[any_spec] * 3,
             out_specs=(vmem_spec, vmem_spec),
             scratch_shapes=[
-                pltpu.VMEM((groups, steps, LANES), f32),
-                pltpu.VMEM((groups, steps, LANES), f32),
+                pltpu.VMEM((2, 2, groups // 2, steps, LANES), f32),
                 pltpu.VMEM((sites, modes), f32),
                 pltpu.VMEM((sites, modes), jnp.bfloat16),
                 pltpu.VMEM((sites, modes), jnp.bfloat16),
@@ -396,20 +391,19 @@
                 pltpu.VMEM((3, SUB, modes), f32),
                 pltpu.VMEM((3, SUB, modes), f32),
                 pltpu.VMEM((PIECES, 3, width, LANES), f32),
-                pltpu.VMEM((PIECES, 2 * nx, 3, width, LANES), f32),
-                pltpu.VMEM((PIECES, nz, 3, width, LANES), f32),
-                pltpu.VMEM((PIECES, ny, 3, width, LANES), f32),
+                pltpu.VMEM((PIECES, 2 * nx + nz + ny, 3, width, LANES), f32),
                 pltpu.VMEM((PIECES, 2, 3, width, LANES), f32),
                 pltpu.VMEM((PIECES, 2, width, LANES), f32),
                 pltpu.VMEM((PIECES, 2, width, LANES), f32),
                 pltpu.VMEM((4 * steps, modes), jnp.bfloat16),
                 pltpu.VMEM((4, sites // LANES, steps, LANES), f32),
-                dma((2, PIECES)),
+                dma((2,)),
                 dma,
-                dma((PIECES + 1,)),
-                dma((PIECES + 1,)),
-                dma((PIECES + 1,)),
-                dma((PIECES + 1,)),
+                dma((PIECES,)),
+                dma((PIECES,)),
+                dma((PIECES,)),
+                dma,
+                dma,
                 pltpu.SemaphoreType.REGULAR,
             ],
             compiler_params=pltpu.CompilerParams(collective_id=0, has_side_effects=True),

time: 27.8 us -> 27.7 us (level)
  no operation moved by 1% of the time
where the time goes in v6:
time: 27.7 us; the launch traced here: 27.5 us
  Pallas kernels  26.1 us (94%)
  other arithmetic  0.71 us (3%)
  between operations  0.64 us (2%)
    pallas_call x1, Pallas kernels, per_device(): pl.pallas_call(functools.partial(kernel, sizes), out_shape=(out, out), in...  26.1 us
    another operation x1, other arithmetic, per_device(): return lax.reduce(fields, (zero, zero), add, (0,))  0.71 us

profile of v6, /device:TPU:1, one launch (start us, length us, event | category | flops | bytes accessed | tf_op | source)
XLA Modules:
  0.0 27.5 jit_solution(8117614736806769582)
XLA Ops:
  0.6 26.1 %shard_map.50 = (f32[2,32,384]{2,1,0:T(8,128)S(1)}, f32[2,32,384]{2,1,0:T(8,128)S(1)}) custom-call(f32[32,1536]{1,0:T(8,128)} %c_hbm.1, f32[32,1536]{1,0:T(8,128)} %w_hbm.1, f32[384,1536]{1,0:T(8,128)} %b_hbm.1), custom_call_target="tpu_custom_call" | custom-call | tf_op jit(solution)/shard_map/pallas_call | solution.py:380
  26.8 0.7 %reduce.15 = (f32[32,384]{1,0:T(8,128)}, f32[32,384]{1,0:T(8,128)}) reduce(f32[2,32,384]{2,1,0:T(8,128)S(1)} %get-tuple-element.4, f32[2,32,384]{2,1,0:T(8,128)S(1)} %get-tuple-element.5, f32[]{:T(128)} %constant.0.clone.1, f32[]{:T(128)} %constant.0.clone.1), dimensions={0}, to_apply=%region_0.0 | reduce | flops 24576 | bytes 294920 | tf_op jit(solution)/shard_map/reduce | solution.py:416

commit v7 on v6

--- a/solution.py
+++ b/solution.py
@@ -197,8 +197,8 @@
     @pl.when(h == 1)
     def _():
         def spread(pieces, place, received, dests, peer_of):
-            for i in dests:
-                for c in pieces:
+            for c in pieces:
+                for i in dests:
                     peer, known = peer_of(i)
                     send(nets.at[c, place], nets.at[c, place], net_sent, received.at[c], peer, known)
 
@@ -227,11 +227,8 @@
             put(c, at_z + z, tree(x_nets[c]))
             spread_z((0,), (c,))
         row_sides = [around(x_nets[c], x) for c in pieces]
-        weigh_some(0, 6)
-        spread_z((1,))
-        weigh_some(1, 6)
-        spread_z(range(2, nz // 2))
-        weigh_some(2, 6)
+        spread_z(range(1, nz // 2))
+        weigh_some(0, 2)
         spread_z(range(nz // 2, nz))
         for c in pieces:
             await_bytes(nets.at[c, pl.ds(at_z, nz - 1)], z_recv.at[c])
@@ -247,13 +244,9 @@
                 sides[c, 0, p] = before[p]
                 sides[c, 1, p] = after[p]
         near = near_first(ny)
-        spread_y(near[1:2])
-        weigh_some(3, 6)
-        spread_y(near[2:4])
-        weigh_some(4, 6)
-        spread_y(near[4:6])
-        weigh_some(5, 6)
-        spread_y(near[6:])
+        spread_y(near[1:4])
+        weigh_some(1, 2)
+        spread_y(near[4:])
 
     @pl.when(h == 0)
     def _():
@@ -322,8 +315,8 @@
         def _():
             await_bytes(d_buf.at[c], x_recv.at[c])
 
-    def multiply(i):
-        at = slice(i * half * LANES, (i + 1) * half * LANES)
+    def multiply(first, end):
+        at = slice(first * width * LANES, end * width * LANES)
         with_high = lax.dot_general(stack[:, at], w_high[:, at], contract, preferred_element_type=jnp.float32)
         with_low = lax.dot_general(
             stack[0 : 2 * rows, at], w_low[:, at], contract, preferred_element_type=jnp.float32
@@ -335,8 +328,8 @@
         learn(c)
         for k in range(c * width // span, (c + 1) * width // span):
             finish(k)
-        if (c + 1) * width % half == 0:
-            new = multiply(c * width // half)
+        if c in (0, PIECES - 1):
+            new = multiply(min(c, 1), c + 1)
             parts = new if parts is None else tuple(o + n for o, n in zip(parts, new))
 
     for o, ref in enumerate((var_ref, lag_ref)):

time: 27.7 us -> 27.5 us (level)
  no operation moved by 1% of the time
where the time goes in v7:
time: 27.5 us; the launch traced here: 27.3 us
  Pallas kernels  25.9 us (94%)
  other arithmetic  0.71 us (3%)
  between operations  0.64 us (2%)
    pallas_call x1, Pallas kernels, per_device(): pl.pallas_call(functools.partial(kernel, sizes), out_shape=(out, out), in...  25.9 us
    another operation x1, other arithmetic, per_device(): return lax.reduce(fields, (zero, zero), add, (0,))  0.71 us

profile of v7, /device:TPU:1, one launch (start us, length us, event | category | flops | bytes accessed | tf_op | source)
XLA Modules:
  0.0 27.3 jit_solution(735838315926924312)
XLA Ops:
  0.6 25.9 %shard_map.50 = (f32[2,32,384]{2,1,0:T(8,128)S(1)}, f32[2,32,384]{2,1,0:T(8,128)S(1)}) custom-call(f32[32,1536]{1,0:T(8,128)} %c_hbm.1, f32[32,1536]{1,0:T(8,128)} %w_hbm.1, f32[384,1536]{1,0:T(8,128)} %b_hbm.1), custom_call_target="tpu_custom_call" | custom-call | tf_op jit(solution)/shard_map/pallas_call | solution.py:373
  26.6 0.7 %reduce.15 = (f32[32,384]{1,0:T(8,128)}, f32[32,384]{1,0:T(8,128)}) reduce(f32[2,32,384]{2,1,0:T(8,128)S(1)} %get-tuple-element.4, f32[2,32,384]{2,1,0:T(8,128)S(1)} %get-tuple-element.5, f32[]{:T(128)} %constant.0.clone.1, f32[]{:T(128)} %constant.0.clone.1), dimensions={0}, to_apply=%region_0.0 | reduce | flops 24576 | bytes 294920 | tf_op jit(solution)/shard_map/reduce | solution.py:409

commit v8 on v7

--- a/solution.py
+++ b/solution.py
@@ -11,7 +11,7 @@
 MESH = pl.DeviceIdType.MESH
 AXES = ("y", "z", "x", "c")
 LANES = 128
-PIECES = 4
+PIECES = 3
 SUB = 8
 
 
@@ -66,7 +66,7 @@
     groups = modes // LANES
     sites = b_v.shape[0]
     width = groups // PIECES
-    span = 3 if width % 3 == 0 else width
+    span = 3 if width % 3 == 0 else 2
     chunk = span * LANES
     n_chunks = modes // chunk
     pieces = range(PIECES)

time: 27.5 us -> 27.4 us (level)
  no operation moved by 1% of the time
where the time goes in v8:
time: 27.4 us; the launch traced here: 27.2 us
  Pallas kernels  25.9 us (95%)
  other arithmetic  0.71 us (3%)
  between operations  0.64 us (2%)
    pallas_call x1, Pallas kernels, per_device(): pl.pallas_call(functools.partial(kernel, sizes), out_shape=(out, out), in...  25.9 us
    another operation x1, other arithmetic, per_device(): return lax.reduce(fields, (zero, zero), add, (0,))  0.71 us

profile of v8, /device:TPU:1, one launch (start us, length us, event | category | flops | bytes accessed | tf_op | source)
XLA Modules:
  0.0 27.2 jit_solution(3530915768692712012)
XLA Ops:
  0.6 25.9 %shard_map.50 = (f32[2,32,384]{2,1,0:T(8,128)S(1)}, f32[2,32,384]{2,1,0:T(8,128)S(1)}) custom-call(f32[32,1536]{1,0:T(8,128)} %c_hbm.1, f32[32,1536]{1,0:T(8,128)} %w_hbm.1, f32[384,1536]{1,0:T(8,128)} %b_hbm.1), custom_call_target="tpu_custom_call" | custom-call | tf_op jit(solution)/shard_map/pallas_call | solution.py:373
  26.5 0.7 %reduce.15 = (f32[32,384]{1,0:T(8,128)}, f32[32,384]{1,0:T(8,128)}) reduce(f32[2,32,384]{2,1,0:T(8,128)S(1)} %get-tuple-element.4, f32[2,32,384]{2,1,0:T(8,128)S(1)} %get-tuple-element.5, f32[]{:T(128)} %constant.0.clone.1, f32[]{:T(128)} %constant.0.clone.1), dimensions={0}, to_apply=%region_0.0 | reduce | flops 24576 | bytes 294920 | tf_op jit(solution)/shard_map/reduce | solution.py:409
